TPU v7x, 128 devices: a whole 4x4x4 slice. The times are simulated.
128 devices in a mesh: row: 8 (over z, core), col: 16 (over y, x).
Axes of the slice: x: 4, y: 4, z: 4, core: 2. Of those that a mesh axis runs over, the one named last changes fastest.
Arguments:
- node_lat: bfloat16 [65536, 512], P(('row', 'col')), may hold values from -6 to 6
- edge_lat: bfloat16 [524288, 512], P(('row', 'col')), may hold values from -6 to 6
- near_send: int32 [128, 2, 64], P(('row', 'col')), may hold values from 0 to 511, as said below
- far_send: int32 [128, 128, 8], P(('row', 'col')), may hold values from -1 to 511, as said below
- edge_sender: int32 [524288], P(('row', 'col')), may hold values from 0 to 1663, as said below
- edge_receiver: int32 [524288], P(('row', 'col')), may hold values from 0 to 511
- edge_inner: bfloat16 [1536, 512], replicated, may hold values from -0.15625 to 0.15625
- edge_bias: float32 [512], replicated, may hold values from -3 to 3
- edge_outer: bfloat16 [512, 512], replicated, may hold values from -0.25 to 0.25
- edge_offset: float32 [512], replicated, may hold values from -3 to 3
- edge_gain: float32 [512], replicated, may hold values from 0.5 to 1.5
- edge_shift: float32 [512], replicated, may hold values from -2 to 2
- node_inner: bfloat16 [1024, 512], replicated, may hold values from -0.1875 to 0.1875
- node_bias: float32 [512], replicated, may hold values from -3 to 3
- node_outer: bfloat16 [512, 512], replicated, may hold values from -0.25 to 0.25
- node_offset: float32 [512], replicated, may hold values from -3 to 3
- node_gain: float32 [512], replicated, may hold values from 0.5 to 1.5
- node_shift: float32 [512], replicated, may hold values from -2 to 2
Outputs:
- edge_new: bfloat16 [524288, 512], P(('row', 'col'))
- node_new: bfloat16 [65536, 512], P(('row', 'col'))
Inputs may be any that keep to these rules, and one draw needn't show every extreme that they name: `near_send`: rows of the sending device's own nodes. `far_send`: in each pair of devices the filled slots come first; a device sends nothing to itself; every device receives 8 filled slots from some one device. `edge_sender`: points only at own nodes, near rows or filled far slots of the lookup table.
All inputs are finite; a program needn't handle non-finite values.
Results may differ from a plain program's by a relative error of at most 0.008.
Values may be sent and summed in bfloat16 or wider, within the bound.
A program may use at most 64 MiB of HBM per device.

v0:
```python
import jax
import jax.numpy as jnp
from jax import lax
from jax.sharding import PartitionSpec as P


def from_behind(shard, axis, by):
    devices = lax.axis_size(axis)
    return lax.ppermute(shard, axis, [(i, (i + by) % devices) for i in range(devices)])


def layer_norm(values, gain_vec, shift_vec):
    centre = jnp.mean(values, axis=-1, keepdims=True)
    spread = jnp.mean(jnp.square(values - centre), axis=-1, keepdims=True)
    return (values - centre) * lax.rsqrt(spread + 1e-05) * gain_vec + shift_vec


def shards(
    node_lat,
    edge_lat,
    near_send,
    far_send,
    edge_sender,
    edge_receiver,
    edge_inner,
    edge_bias,
    edge_outer,
    edge_offset,
    edge_gain,
    edge_shift,
    node_inner,
    node_bias,
    node_outer,
    node_offset,
    node_gain,
    node_shift,
):
    lat_width = node_lat.shape[1]
    node_count = node_lat.shape[0]
    edge_count = edge_lat.shape[0]
    to_east = node_lat[near_send[0, 0]]
    to_west = node_lat[near_send[0, 1]]
    far_picks = far_send[0]
    far_rows = node_lat[jnp.maximum(far_picks, 0)]
    far_rows = jnp.where((far_picks >= 0)[..., None], far_rows, jnp.zeros_like(far_rows))
    from_west = from_behind(to_east, "col", 1)
    from_east = from_behind(to_west, "col", -1)
    far_in = lax.all_to_all(far_rows, ("row", "col"), split_axis=0, concat_axis=0, tiled=True)
    lookup_table = jnp.concatenate(
        [node_lat, from_west, from_east, far_in.reshape(-1, lat_width)], axis=0
    )
    table_ids = jnp.arange(lookup_table.shape[0], dtype=jnp.int32)
    node_ids = jnp.arange(node_count, dtype=jnp.int32)
    block_rows = min(512, edge_count)
    block_count = edge_count // block_rows
    edge_blocks = edge_lat.reshape(block_count, block_rows, lat_width)
    sender_blocks = edge_sender.reshape(block_count, block_rows)
    receiver_blocks = edge_receiver.reshape(block_count, block_rows)

    def one_block(incoming_sum, block):
        edge_rows, sender_ids, receiver_ids = block
        sender_hot = (sender_ids[:, None] == table_ids[None, :]).astype(jnp.bfloat16)
        receiver_hot = (receiver_ids[:, None] == node_ids[None, :]).astype(jnp.bfloat16)
        sender_rows = jnp.dot(sender_hot, lookup_table, preferred_element_type=jnp.float32).astype(
            jnp.bfloat16
        )
        receiver_rows = jnp.dot(receiver_hot, node_lat, preferred_element_type=jnp.float32).astype(
            jnp.bfloat16
        )
        joined = jnp.concatenate([edge_rows, sender_rows, receiver_rows], axis=1)
        edge_hidden = jax.nn.silu(
            jnp.dot(joined, edge_inner, preferred_element_type=jnp.float32) + edge_bias
        ).astype(jnp.bfloat16)
        edge_post = (
            jnp.dot(edge_hidden, edge_outer, preferred_element_type=jnp.float32) + edge_offset
        )
        message = layer_norm(edge_post, edge_gain, edge_shift).astype(jnp.bfloat16)
        edge_out = (edge_rows.astype(jnp.float32) + message.astype(jnp.float32)).astype(
            jnp.bfloat16
        )
        added = lax.dot_general(
            receiver_hot, message, (((0,), (0,)), ((), ())), preferred_element_type=jnp.float32
        )
        return (incoming_sum + added, edge_out)

    start_sum = jnp.zeros((node_count, lat_width), jnp.float32)
    incoming_sum, edge_out = lax.scan(
        one_block, start_sum, (edge_blocks, sender_blocks, receiver_blocks)
    )
    edge_new = edge_out.reshape(edge_count, lat_width)
    incoming = incoming_sum.astype(jnp.bfloat16)
    node_joined = jnp.concatenate([node_lat, incoming], axis=1)
    node_hidden = jax.nn.silu(
        jnp.dot(node_joined, node_inner, preferred_element_type=jnp.float32) + node_bias
    ).astype(jnp.bfloat16)
    node_post = jnp.dot(node_hidden, node_outer, preferred_element_type=jnp.float32) + node_offset
    node_new = (node_lat.astype(jnp.float32) + layer_norm(node_post, node_gain, node_shift)).astype(
        jnp.bfloat16
    )
    return (edge_new, node_new)


def solution(mesh):
    in_specs = (
        P(("row", "col"), None),
        P(("row", "col"), None),
        P(("row", "col"), None, None),
        P(("row", "col"), None, None),
        P(("row", "col")),
        P(("row", "col")),
        P(),
        P(),
        P(),
        P(),
        P(),
        P(),
        P(),
        P(),
        P(),
        P(),
        P(),
        P(),
    )
    out_specs = (P(("row", "col"), None), P(("row", "col"), None))
    return jax.shard_map(shards, mesh=mesh, in_specs=in_specs, out_specs=out_specs, check_vma=False)
```

profile of v0, /device:TPU:1, one launch (start us, length us, event | category | flops | bytes accessed | tf_op | source)
XLA Modules:
  0.0 174.1 jit_solution(92128698626162070)
XLA Ops:
  2.4 5.1 %gather_fusion.2 = bf16[1024,512]{1,0:T(8,128)(2,1)S(1)} fusion(bf16[512,512]{1,0:T(8,128)(2,1)} %param.20, s32[1024]{0:T(1024)S(1)} %broadcast_clamp_fusion), kind=kCustom, calls=%fused_computation.2 | custom fusion | bytes 2101248 | tf_op jit(solution)/shard_map/gather | solution.py:44
  7.6 1.2 bitcast_select_fusion
  8.8 11.5 %all-to-all-start = ((bf16[128,8,512]{2,1,0:T(8,128)(2,1)}), bf16[128,8,512]{2,1,0:T(8,128)(2,1)S(1)}, u32[]{:S(2)}, u32[]{:S(2)}) async-start(bf16[128,8,512]{2,1,0:T(8,128)(2,1)} %bitcast_select_fusion), calls=%async_computation | async-start | bytes 2097152 | tf_op jit(solution)/shard_map/all_to_all | solution.py:48
  21.1 4.9 %collective-permute-start.1 = (bf16[64,512]{1,0:T(8,128)(2,1)S(1)}, bf16[64,512]{1,0:T(8,128)(2,1)S(1)}, u32[]{:S(2)}, u32[]{:S(2)}) collective-permute-start(bf16[64,512]{1,0:T(8,128)(2,1)S(1)} %gather_fusion.1), channel_id=1, source_target_pairs={{0,15},{1,0},{2,1},{3,2},{4,3},{5,4},{6,5},{7,6},{8,7},{9,8},{10,9... | collective-permute-start | bytes 196616 | tf_op jit(solution)/shard_map/ppermute | solution.py:9
  27.8 6.5 %collective-permute-done.1 = bf16[64,512]{1,0:T(8,128)(2,1)S(1)} collective-permute-done((bf16[64,512]{1,0:T(8,128)(2,1)S(1)}, bf16[64,512]{1,0:T(8,128)(2,1)S(1)}, u32[]{:S(2)}, u32[]{:S(2)}) %collective-permute-start.1) | collective-permute-done | bytes 65568 | tf_op jit(solution)/shard_map/ppermute | solution.py:9
  34.3 3.5 %collective-permute-done = bf16[64,512]{1,0:T(8,128)(2,1)S(1)} collective-permute-done((bf16[64,512]{1,0:T(8,128)(2,1)S(1)}, bf16[64,512]{1,0:T(8,128)(2,1)S(1)}, u32[]{:S(2)}, u32[]{:S(2)}) %collective-permute-start) | collective-permute-done | bytes 65568 | tf_op jit(solution)/shard_map/ppermute | solution.py:9
  37.7 1.6 all-to-all-done
  39.4 1.3 pad_maximum_fusion
  40.7 127.2 %while.13 = (s32[]{:T(128)}, f32[512,512]{1,0:T(8,128)}, bf16[8,512,512]{2,1,0:T(8,128)(2,1)}, s32[8,512]{1,0:T(8,128)S(1)}, bf16[8,512,512]{2,1,0:T(8,128)(2,1)...) while((s32[]{:T(128)}, f32[512,512]{1,0:T(8,128)}, ...), condition=%wide.region_3.4_spmd.clone, body=%wide.region_0.3_spmd.clone.sunk | while | flops 2496987648 | bytes 18530484 | solution.py:87
  40.8 1.4 convolution_convert_fusion.2
  42.2 3.6 %fusion.71 = bf16[512,512]{0,1:T(8,128)(2,1)} fusion(bf16[1664,512]{1,0:T(8,128)(2,1)} %get-tuple-element.321, s32[512]{0:T(512)S(1)} %bitcast.50), kind=kOutput, calls=%fused_computation.18.clone.1 | convolution fusion | flops 873529344 | bytes 2230272 | tf_op jit(solution)/shard_map/while/body/eval_jaxpr/dot_general | solution.py:64
  45.8 1.1 constant_dynamic-slice_fusion.6
  47.1 3.4 %fusion.72 = (f32[512]{0:T(512)S(1)}, f32[512,512]{0,1:T(8,128)S(1)}) fusion(f32[512]{0:T(512)S(1)} %get-tuple-element.326, bf16[512,512]{1,0:T(8,128)(2,1)} %get-tuple-element.325, bf16[1536,512]{1,0:T(8,128)(2,1)} %get-tuple-element.323, bf16[512,512]{0,1:T(8,128)(2,1)} %convolution_convert_fusion.2, bf16[512,512]{0,1:T(8,128)(2,1)} %fusion.71, ...), kind=kOutput, calls=%fused_computation.63.clone.1 | convolution fusion | flops 1080557056 | bytes 4724736 | tf_op jit(solution)/shard_map/while/body/eval_jaxpr/dot_general | solution.py:75
  50.7 1.7 convolution_add_fusion.5
  52.4 1.1 fusion.73
  53.5 1.3 copy.36
  55.6 1.4 convolution_convert_fusion.2
  57.0 3.6 %fusion.71 = bf16[512,512]{0,1:T(8,128)(2,1)} fusion(bf16[1664,512]{1,0:T(8,128)(2,1)} %get-tuple-element.321, s32[512]{0:T(512)S(1)} %bitcast.50), kind=kOutput, calls=%fused_computation.18.clone.1 | convolution fusion | flops 873529344 | bytes 2230272 | tf_op jit(solution)/shard_map/while/body/eval_jaxpr/dot_general | solution.py:64
  60.6 1.1 constant_dynamic-slice_fusion.6
  61.9 3.4 %fusion.72 = (f32[512]{0:T(512)S(1)}, f32[512,512]{0,1:T(8,128)S(1)}) fusion(f32[512]{0:T(512)S(1)} %get-tuple-element.326, bf16[512,512]{1,0:T(8,128)(2,1)} %get-tuple-element.325, bf16[1536,512]{1,0:T(8,128)(2,1)} %get-tuple-element.323, bf16[512,512]{0,1:T(8,128)(2,1)} %convolution_convert_fusion.2, bf16[512,512]{0,1:T(8,128)(2,1)} %fusion.71, ...), kind=kOutput, calls=%fused_computation.63.clone.1 | convolution fusion | flops 1080557056 | bytes 4724736 | tf_op jit(solution)/shard_map/while/body/eval_jaxpr/dot_general | solution.py:75
  65.5 2.9 %convolution_add_fusion.5 = f32[512,512]{1,0:T(8,128)} fusion(f32[512,512]{1,0:T(8,128)} %get-tuple-element.300, s32[512]{0:T(512)S(1)} %bitcast.49, pred[]{:T(512)S(6)} %compare.3, f32[512,512]{0,1:T(8,128)S(1)} %get-tuple-element.281, f32[512]{0:T(512)S(1)} %get-tuple-element.328, f32[512]{0:T(512)S(1)} %get-tuple-element.327, ...), kind=kOutput, calls=%fused_computation.14.clone.1 | convolution fusion | flops 270794752 | bytes 3155969 | tf_op jit(solution)/shard_map/while/body/eval_jaxpr/dot_general | solution.py:81
  68.4 1.1 fusion.73
  69.5 1.3 copy.36
  71.6 1.4 convolution_convert_fusion.2
  73.1 3.6 %fusion.71 = bf16[512,512]{0,1:T(8,128)(2,1)} fusion(bf16[1664,512]{1,0:T(8,128)(2,1)} %get-tuple-element.321, s32[512]{0:T(512)S(1)} %bitcast.50), kind=kOutput, calls=%fused_computation.18.clone.1 | convolution fusion | flops 873529344 | bytes 2230272 | tf_op jit(solution)/shard_map/while/body/eval_jaxpr/dot_general | solution.py:64
  76.6 1.1 constant_dynamic-slice_fusion.6
  77.9 3.4 %fusion.72 = (f32[512]{0:T(512)S(1)}, f32[512,512]{0,1:T(8,128)S(1)}) fusion(f32[512]{0:T(512)S(1)} %get-tuple-element.326, bf16[512,512]{1,0:T(8,128)(2,1)} %get-tuple-element.325, bf16[1536,512]{1,0:T(8,128)(2,1)} %get-tuple-element.323, bf16[512,512]{0,1:T(8,128)(2,1)} %convolution_convert_fusion.2, bf16[512,512]{0,1:T(8,128)(2,1)} %fusion.71, ...), kind=kOutput, calls=%fused_computation.63.clone.1 | convolution fusion | flops 1080557056 | bytes 4724736 | tf_op jit(solution)/shard_map/while/body/eval_jaxpr/dot_general | solution.py:75
  81.6 2.9 %convolution_add_fusion.5 = f32[512,512]{1,0:T(8,128)} fusion(f32[512,512]{1,0:T(8,128)} %get-tuple-element.300, s32[512]{0:T(512)S(1)} %bitcast.49, pred[]{:T(512)S(6)} %compare.3, f32[512,512]{0,1:T(8,128)S(1)} %get-tuple-element.281, f32[512]{0:T(512)S(1)} %get-tuple-element.328, f32[512]{0:T(512)S(1)} %get-tuple-element.327, ...), kind=kOutput, calls=%fused_computation.14.clone.1 | convolution fusion | flops 270794752 | bytes 3155969 | tf_op jit(solution)/shard_map/while/body/eval_jaxpr/dot_general | solution.py:81
  84.5 1.1 fusion.73
  85.6 1.3 copy.36
  87.7 1.4 convolution_convert_fusion.2
  89.1 3.6 %fusion.71 = bf16[512,512]{0,1:T(8,128)(2,1)} fusion(bf16[1664,512]{1,0:T(8,128)(2,1)} %get-tuple-element.321, s32[512]{0:T(512)S(1)} %bitcast.50), kind=kOutput, calls=%fused_computation.18.clone.1 | convolution fusion | flops 873529344 | bytes 2230272 | tf_op jit(solution)/shard_map/while/body/eval_jaxpr/dot_general | solution.py:64
  92.7 1.1 constant_dynamic-slice_fusion.6
  94.0 3.4 %fusion.72 = (f32[512]{0:T(512)S(1)}, f32[512,512]{0,1:T(8,128)S(1)}) fusion(f32[512]{0:T(512)S(1)} %get-tuple-element.326, bf16[512,512]{1,0:T(8,128)(2,1)} %get-tuple-element.325, bf16[1536,512]{1,0:T(8,128)(2,1)} %get-tuple-element.323, bf16[512,512]{0,1:T(8,128)(2,1)} %convolution_convert_fusion.2, bf16[512,512]{0,1:T(8,128)(2,1)} %fusion.71, ...), kind=kOutput, calls=%fused_computation.63.clone.1 | convolution fusion | flops 1080557056 | bytes 4724736 | tf_op jit(solution)/shard_map/while/body/eval_jaxpr/dot_general | solution.py:75
  97.6 2.9 %convolution_add_fusion.5 = f32[512,512]{1,0:T(8,128)} fusion(f32[512,512]{1,0:T(8,128)} %get-tuple-element.300, s32[512]{0:T(512)S(1)} %bitcast.49, pred[]{:T(512)S(6)} %compare.3, f32[512,512]{0,1:T(8,128)S(1)} %get-tuple-element.281, f32[512]{0:T(512)S(1)} %get-tuple-element.328, f32[512]{0:T(512)S(1)} %get-tuple-element.327, ...), kind=kOutput, calls=%fused_computation.14.clone.1 | convolution fusion | flops 270794752 | bytes 3155969 | tf_op jit(solution)/shard_map/while/body/eval_jaxpr/dot_general | solution.py:81
  100.5 1.1 fusion.73
  101.6 1.3 copy.36
  103.7 1.4 convolution_convert_fusion.2
  105.2 3.6 %fusion.71 = bf16[512,512]{0,1:T(8,128)(2,1)} fusion(bf16[1664,512]{1,0:T(8,128)(2,1)} %get-tuple-element.321, s32[512]{0:T(512)S(1)} %bitcast.50), kind=kOutput, calls=%fused_computation.18.clone.1 | convolution fusion | flops 873529344 | bytes 2230272 | tf_op jit(solution)/shard_map/while/body/eval_jaxpr/dot_general | solution.py:64
  108.7 1.1 constant_dynamic-slice_fusion.6
  110.0 3.4 %fusion.72 = (f32[512]{0:T(512)S(1)}, f32[512,512]{0,1:T(8,128)S(1)}) fusion(f32[512]{0:T(512)S(1)} %get-tuple-element.326, bf16[512,512]{1,0:T(8,128)(2,1)} %get-tuple-element.325, bf16[1536,512]{1,0:T(8,128)(2,1)} %get-tuple-element.323, bf16[512,512]{0,1:T(8,128)(2,1)} %convolution_convert_fusion.2, bf16[512,512]{0,1:T(8,128)(2,1)} %fusion.71, ...), kind=kOutput, calls=%fused_computation.63.clone.1 | convolution fusion | flops 1080557056 | bytes 4724736 | tf_op jit(solution)/shard_map/while/body/eval_jaxpr/dot_general | solution.py:75
  113.7 2.9 %convolution_add_fusion.5 = f32[512,512]{1,0:T(8,128)} fusion(f32[512,512]{1,0:T(8,128)} %get-tuple-element.300, s32[512]{0:T(512)S(1)} %bitcast.49, pred[]{:T(512)S(6)} %compare.3, f32[512,512]{0,1:T(8,128)S(1)} %get-tuple-element.281, f32[512]{0:T(512)S(1)} %get-tuple-element.328, f32[512]{0:T(512)S(1)} %get-tuple-element.327, ...), kind=kOutput, calls=%fused_computation.14.clone.1 | convolution fusion | flops 270794752 | bytes 3155969 | tf_op jit(solution)/shard_map/while/body/eval_jaxpr/dot_general | solution.py:81
  116.6 1.1 fusion.73
  117.7 1.3 copy.36
  119.8 1.4 convolution_convert_fusion.2
  121.2 3.6 %fusion.71 = bf16[512,512]{0,1:T(8,128)(2,1)} fusion(bf16[1664,512]{1,0:T(8,128)(2,1)} %get-tuple-element.321, s32[512]{0:T(512)S(1)} %bitcast.50), kind=kOutput, calls=%fused_computation.18.clone.1 | convolution fusion | flops 873529344 | bytes 2230272 | tf_op jit(solution)/shard_map/while/body/eval_jaxpr/dot_general | solution.py:64
  126.1 3.4 %fusion.72 = (f32[512]{0:T(512)S(1)}, f32[512,512]{0,1:T(8,128)S(1)}) fusion(f32[512]{0:T(512)S(1)} %get-tuple-element.326, bf16[512,512]{1,0:T(8,128)(2,1)} %get-tuple-element.325, bf16[1536,512]{1,0:T(8,128)(2,1)} %get-tuple-element.323, bf16[512,512]{0,1:T(8,128)(2,1)} %convolution_convert_fusion.2, bf16[512,512]{0,1:T(8,128)(2,1)} %fusion.71, ...), kind=kOutput, calls=%fused_computation.63.clone.1 | convolution fusion | flops 1080557056 | bytes 4724736 | tf_op jit(solution)/shard_map/while/body/eval_jaxpr/dot_general | solution.py:75
  129.7 2.9 %convolution_add_fusion.5 = f32[512,512]{1,0:T(8,128)} fusion(f32[512,512]{1,0:T(8,128)} %get-tuple-element.300, s32[512]{0:T(512)S(1)} %bitcast.49, pred[]{:T(512)S(6)} %compare.3, f32[512,512]{0,1:T(8,128)S(1)} %get-tuple-element.281, f32[512]{0:T(512)S(1)} %get-tuple-element.328, f32[512]{0:T(512)S(1)} %get-tuple-element.327, ...), kind=kOutput, calls=%fused_computation.14.clone.1 | convolution fusion | flops 270794752 | bytes 3155969 | tf_op jit(solution)/shard_map/while/body/eval_jaxpr/dot_general | solution.py:81
  132.7 1.1 fusion.73
  133.7 1.3 copy.36
  135.8 1.4 convolution_convert_fusion.2
  137.3 3.6 %fusion.71 = bf16[512,512]{0,1:T(8,128)(2,1)} fusion(bf16[1664,512]{1,0:T(8,128)(2,1)} %get-tuple-element.321, s32[512]{0:T(512)S(1)} %bitcast.50), kind=kOutput, calls=%fused_computation.18.clone.1 | convolution fusion | flops 873529344 | bytes 2230272 | tf_op jit(solution)/shard_map/while/body/eval_jaxpr/dot_general | solution.py:64
  142.1 3.4 %fusion.72 = (f32[512]{0:T(512)S(1)}, f32[512,512]{0,1:T(8,128)S(1)}) fusion(f32[512]{0:T(512)S(1)} %get-tuple-element.326, bf16[512,512]{1,0:T(8,128)(2,1)} %get-tuple-element.325, bf16[1536,512]{1,0:T(8,128)(2,1)} %get-tuple-element.323, bf16[512,512]{0,1:T(8,128)(2,1)} %convolution_convert_fusion.2, bf16[512,512]{0,1:T(8,128)(2,1)} %fusion.71, ...), kind=kOutput, calls=%fused_computation.63.clone.1 | convolution fusion | flops 1080557056 | bytes 4724736 | tf_op jit(solution)/shard_map/while/body/eval_jaxpr/dot_general | solution.py:75
  145.8 2.9 %convolution_add_fusion.5 = f32[512,512]{1,0:T(8,128)} fusion(f32[512,512]{1,0:T(8,128)} %get-tuple-element.300, s32[512]{0:T(512)S(1)} %bitcast.49, pred[]{:T(512)S(6)} %compare.3, f32[512,512]{0,1:T(8,128)S(1)} %get-tuple-element.281, f32[512]{0:T(512)S(1)} %get-tuple-element.328, f32[512]{0:T(512)S(1)} %get-tuple-element.327, ...), kind=kOutput, calls=%fused_computation.14.clone.1 | convolution fusion | flops 270794752 | bytes 3155969 | tf_op jit(solution)/shard_map/while/body/eval_jaxpr/dot_general | solution.py:81
  148.7 1.1 fusion.73
  149.8 1.3 copy.36
  151.9 1.4 convolution_convert_fusion.2
  153.3 3.6 %fusion.71 = bf16[512,512]{0,1:T(8,128)(2,1)} fusion(bf16[1664,512]{1,0:T(8,128)(2,1)} %get-tuple-element.321, s32[512]{0:T(512)S(1)} %bitcast.50), kind=kOutput, calls=%fused_computation.18.clone.1 | convolution fusion | flops 873529344 | bytes 2230272 | tf_op jit(solution)/shard_map/while/body/eval_jaxpr/dot_general | solution.py:64
  158.2 3.4 %fusion.72 = (f32[512]{0:T(512)S(1)}, f32[512,512]{0,1:T(8,128)S(1)}) fusion(f32[512]{0:T(512)S(1)} %get-tuple-element.326, bf16[512,512]{1,0:T(8,128)(2,1)} %get-tuple-element.325, bf16[1536,512]{1,0:T(8,128)(2,1)} %get-tuple-element.323, bf16[512,512]{0,1:T(8,128)(2,1)} %convolution_convert_fusion.2, bf16[512,512]{0,1:T(8,128)(2,1)} %fusion.71, ...), kind=kOutput, calls=%fused_computation.63.clone.1 | convolution fusion | flops 1080557056 | bytes 4724736 | tf_op jit(solution)/shard_map/while/body/eval_jaxpr/dot_general | solution.py:75
  161.8 2.9 %convolution_add_fusion.5 = f32[512,512]{1,0:T(8,128)} fusion(f32[512,512]{1,0:T(8,128)} %get-tuple-element.300, s32[512]{0:T(512)S(1)} %bitcast.49, pred[]{:T(512)S(6)} %compare.3, f32[512,512]{0,1:T(8,128)S(1)} %get-tuple-element.281, f32[512]{0:T(512)S(1)} %get-tuple-element.328, f32[512]{0:T(512)S(1)} %get-tuple-element.327, ...), kind=kOutput, calls=%fused_computation.14.clone.1 | convolution fusion | flops 270794752 | bytes 3155969 | tf_op jit(solution)/shard_map/while/body/eval_jaxpr/dot_general | solution.py:81
  164.8 1.1 fusion.73
  165.8 1.3 copy.36
  167.9 2.1 %convert_element_type.36 = bf16[512,512]{1,0:T(8,128)(2,1)} convert(f32[512,512]{1,0:T(8,128)} %get-tuple-element.86) | non-fusion elementwise | flops 262144 | bytes 1572864 | tf_op jit(solution)/shard_map/convert_element_type | solution.py:91
  170.0 2.5 %fusion.47 = (f32[512]{0:T(512)S(1)}, f32[512,512]{0,1:T(8,128)S(1)}) fusion(f32[512]{0:T(512)S(1)} %copy-done.12, bf16[512,512]{1,0:T(8,128)(2,1)} %param.34, bf16[1024,512]{1,0:T(8,128)(2,1)S(1)} %copy-done, bf16[512,512]{1,0:T(8,128)(2,1)} %convert_element_type.36, bf16[512,512]{1,0:T(8,128)(2,1)S(1)} %get-tuple-element.331, f32[512]{0:T(512)S(1)} %copy-done.13), kind=kOutput, calls=%fused_computation.64 | convolution fusion | flops 809500160 | bytes 3676160 | tf_op jit(solution)/shard_map/dot_general | solution.py:96
  (101 shorter events, 19.1 us)
Async XLA Ops:
  0.6 169.4 %copy-start = (bf16[1024,512]{1,0:T(8,128)(2,1)S(1)}, bf16[1024,512]{1,0:T(8,128)(2,1)}, u32[]{:S(2)}) copy-start(bf16[1024,512]{1,0:T(8,128)(2,1)} %param.32) | copy-start | bytes 3145732
  7.6 12.7 %copy-start.9 = (s32[1,2,64]{2,1,0:T(2,128)S(1)}, s32[1,2,64]{2,1,0:T(2,128)}, u32[]{:S(2)}) copy-start(s32[1,2,64]{2,1,0:T(2,128)} %param.22) | copy-start | bytes 1540
  7.6 12.8 %copy-start.1 = (bf16[512,512]{1,0:T(8,128)(2,1)S(1)}, bf16[512,512]{1,0:T(8,128)(2,1)}, u32[]{:S(2)}) copy-start(bf16[512,512]{1,0:T(8,128)(2,1)} %param.20) | copy-start | bytes 1572868
  7.6 20.2 %copy-start.5 = (s32[4096]{0:T(1024)S(1)}, s32[4096]{0:T(1024)}, u32[]{:S(2)}) copy-start(s32[4096]{0:T(1024)} %param.25) | copy-start | bytes 49156
  7.6 20.2 %copy-start.6 = (s32[4096]{0:T(1024)S(1)}, s32[4096]{0:T(1024)}, u32[]{:S(2)}) copy-start(s32[4096]{0:T(1024)} %param.24) | copy-start | bytes 49156
  8.8 30.6 %all-to-all-start = ((bf16[128,8,512]{2,1,0:T(8,128)(2,1)}), bf16[128,8,512]{2,1,0:T(8,128)(2,1)S(1)}, u32[]{:S(2)}, u32[]{:S(2)}) async-start(bf16[128,8,512]{2,1,0:T(8,128)(2,1)} %bitcast_select_fusion), calls=%async_computation | async-start | bytes 2097152 | tf_op jit(solution)/shard_map/all_to_all | solution.py:48
  20.3 20.4 %copy-start.3 = (f32[512]{0:T(512)S(1)}, f32[512]{0:T(512)}, u32[]{:S(2)}) copy-start(f32[512]{0:T(512)} %param.30) | copy-start | bytes 6148
  20.3 20.4 %copy-start.4 = (f32[512]{0:T(512)S(1)}, f32[512]{0:T(512)}, u32[]{:S(2)}) copy-start(f32[512]{0:T(512)} %param.31) | copy-start | bytes 6148
  20.3 20.4 %copy-start.10 = (f32[512]{0:T(512)S(1)}, f32[512]{0:T(512)}, u32[]{:S(2)}) copy-start(f32[512]{0:T(512)} %param.27) | copy-start | bytes 6148
  20.3 20.4 %copy-start.11 = (f32[512]{0:T(512)S(1)}, f32[512]{0:T(512)}, u32[]{:S(2)}) copy-start(f32[512]{0:T(512)} %param.29) | copy-start | bytes 6148
  21.1 13.2 %collective-permute-start.1 = (bf16[64,512]{1,0:T(8,128)(2,1)S(1)}, bf16[64,512]{1,0:T(8,128)(2,1)S(1)}, u32[]{:S(2)}, u32[]{:S(2)}) collective-permute-start(bf16[64,512]{1,0:T(8,128)(2,1)S(1)} %gather_fusion.1), channel_id=1, source_target_pairs={{0,15},{1,0},{2,1},{3,2},{4,3},{5,4},{6,5},{7,6},{8,7},{9,8},{10,9... | collective-permute-start | bytes 196616 | tf_op jit(solution)/shard_map/ppermute | solution.py:9
  26.6 11.1 %collective-permute-start = (bf16[64,512]{1,0:T(8,128)(2,1)S(1)}, bf16[64,512]{1,0:T(8,128)(2,1)S(1)}, u32[]{:S(2)}, u32[]{:S(2)}) collective-permute-start(bf16[64,512]{1,0:T(8,128)(2,1)S(1)} %gather_fusion), channel_id=1, source_target_pairs={{0,1},{1,2},{2,3},{3,4},{4,5},{5,6},{6,7},{7,8},{8,9},{9,10},{10,1... | collective-permute-start | bytes 196616 | tf_op jit(solution)/shard_map/ppermute | solution.py:9
  40.7 129.3 %copy-start.12 = (f32[512]{0:T(512)S(1)}, f32[512]{0:T(512)}, u32[]{:S(2)}) copy-start(f32[512]{0:T(512)} %param.35) | copy-start | bytes 6148
  40.7 129.3 %copy-start.13 = (f32[512]{0:T(512)S(1)}, f32[512]{0:T(512)}, u32[]{:S(2)}) copy-start(f32[512]{0:T(512)} %param.33) | copy-start | bytes 6148
  170.0 2.8 %copy-start.2 = (bf16[512,512]{0,1:T(8,128)(2,1)S(1)}, bf16[512,512]{0,1:T(8,128)(2,1)}, u32[]{:S(2)}) copy-start(bf16[512,512]{0,1:T(8,128)(2,1)} %copy.28) | copy-start | bytes 1572868
  170.0 2.8 %copy-start.7 = (f32[512]{0:T(512)S(1)}, f32[512]{0:T(512)}, u32[]{:S(2)}) copy-start(f32[512]{0:T(512)} %param.37) | copy-start | bytes 6148
  170.0 2.8 %copy-start.8 = (f32[512]{0:T(512)S(1)}, f32[512]{0:T(512)}, u32[]{:S(2)}) copy-start(f32[512]{0:T(512)} %param.36) | copy-start | bytes 6148
where the time goes:
time: 176 us; the launch traced here: 174 us
  matrix products  92.2 us (52%)
  local copies, waits for them, and re-layouts  36 us (20%)
  other arithmetic  16.7 us (9%)
  starting transfers between devices  16.4 us (9%)
  waiting for transfers between devices  11.6 us (7%)
    dot_general x8, matrix products, one_block(): jnp.dot(sender_hot, lookup_table, preferred_element_type=jnp.float32)  28.5 us
    dot_general x8, matrix products, one_block(): jnp.dot(edge_hidden, edge_outer, preferred_element_type=jnp.float32)  27.3 us
    dot_general x8, matrix products, one_block(): lax.dot_general(receiver_hot, message, (((0,), (0,)), ((), ())), preferre...  22.3 us
    dynamic_update_slice x16, local copies, waits for them, and re-layouts, shards(): lax.scan(one_block, start_sum, (edge_blocks, sender_blocks, receiver_bloc...  16.7 us
    dot_general x8, matrix products, one_block(): jnp.dot(receiver_hot, node_lat, preferred_element_type=jnp.float32)  11.5 us
    all_to_all x1, starting transfers between devices, shards(): lax.all_to_all(far_rows, ('row', 'col'), split_axis=0, concat_axis=0, til...  11.5 us
    dynamic_slice x24, local copies, waits for them, and re-layouts, shards(): lax.scan(one_block, start_sum, (edge_blocks, sender_blocks, receiver_bloc...  10.4 us
    ppermute x2, waiting for transfers between devices, from_behind(): lax.ppermute(shard, axis, [(i, (i + by) % devices) for i in range(devices)])  9.96 us
  transfers between devices with their start and end apart: 3, of which 3 were waited for; matrix products, arithmetic and copies ran while one was open for 1% of the time, Pallas kernels for 0%

commit v1 on v0

v1 whole, which is shorter than its diff:
```python
import functools

import jax
import jax.numpy as jnp
from jax import lax
from jax.experimental import pallas as pl
from jax.experimental.pallas import tpu as pltpu
from jax.sharding import PartitionSpec as P

F32 = jnp.float32
BF16 = jnp.bfloat16
MESH = pl.DeviceIdType.MESH
LANES = 128


def dot(a, b):
    return jnp.dot(a, b, preferred_element_type=F32)


def silu(x):
    half = 0.5 * x
    return half * jnp.tanh(half) + half


def layer_norm(values, gain, shift):
    centre = jnp.mean(values, axis=-1, keepdims=True)
    off = values - centre
    spread = jnp.mean(off * off, axis=-1, keepdims=True)
    return off * lax.rsqrt(spread + 1e-05) * gain + shift


def put_rows(dst, first, values):
    rows, width = values.shape
    parts = width // LANES
    for k in range(parts):
        part = values[:, k * LANES : (k + 1) * LANES]
        if len(dst.shape) == 3:
            dst[pl.ds(first, rows), k, :] = part
        else:
            dst[pl.ds(first * parts + k, rows, stride=parts), :] = part


def exchange_kernel(
    n_row, n_col, block,
    far_ids, near_ids, receiver, node, edge_hbm, inner, bias,
    pre_hbm, far_out, near_out,
    node_parts, table, picked, far_buf, near_buf, edge_buf, pre_buf,
    far_send_sem, far_recv_sem, near_send_sem, near_recv_sem, edge_sem, pre_sem,
):
    peers = n_row * n_col
    row, col = lax.axis_index("row"), lax.axis_index("col")
    me = row * n_col + col
    nodes, width = node.shape
    edges = edge_hbm.shape[0]
    parts = width // LANES
    slots = far_buf.shape[1]
    halo = near_buf.shape[1]

    edge_copy = pltpu.make_async_copy(edge_hbm, edge_buf, edge_sem)
    edge_copy.start()

    barrier = pltpu.get_barrier_semaphore()

    def greet(i, carry):
        other = lax.rem(me + i, peers)
        pl.semaphore_signal(
            barrier, inc=1, device_id=(lax.div(other, n_col), lax.rem(other, n_col)), device_id_type=MESH
        )
        return carry

    lax.fori_loop(1, peers, greet, 0)

    put_rows(node_parts, 0, node[...].astype(F32))

    def pick(ids):
        for j, row_id in enumerate(ids):
            picked[0, pl.ds(j * parts, parts), :] = node_parts[row_id]
        return [picked[0, pl.ds(k, len(ids), stride=parts), :].astype(BF16) for k in range(parts)]

    def pick_near(i, carry):
        for side in range(2):
            first = pl.multiple_of(i * 16, 16)
            for k, values in enumerate(pick([near_ids[0, side, first + j] for j in range(16)])):
                near_buf[side, pl.ds(first, 16), k * LANES : (k + 1) * LANES] = values
        return carry

    lax.fori_loop(0, halo // 16, pick_near, 0)

    def pick_far(p, carry):
        ids = [jnp.maximum(far_ids[0, p, j], 0) for j in range(slots)]
        for k, values in enumerate(pick(ids)):
            far_buf[p, :, k * LANES : (k + 1) * LANES] = values
        return carry

    lax.fori_loop(0, peers, pick_far, 0)

    pl.semaphore_wait(barrier, peers - 1)

    east = (row, lax.rem(col + 1, n_col))
    west = (row, lax.rem(col + n_col - 1, n_col))
    near_copies = [
        pltpu.make_async_remote_copy(
            src_ref=near_buf.at[side], dst_ref=near_out.at[side],
            send_sem=near_send_sem.at[side], recv_sem=near_recv_sem.at[side],
            device_id=target, device_id_type=MESH,
        )
        for side, target in enumerate((east, west))
    ]
    for copy in near_copies:
        copy.start()

    def send(i, carry):
        other = lax.rem(me + i, peers)
        pltpu.make_async_remote_copy(
            src_ref=far_buf.at[other], dst_ref=far_out.at[me],
            send_sem=far_send_sem, recv_sem=far_recv_sem,
            device_id=(lax.div(other, n_col), lax.rem(other, n_col)), device_id_type=MESH,
        ).start()
        return carry

    lax.fori_loop(1, peers, send, 0)

    put_rows(table, 0, dot(node[...], inner[2 * width :, :]))
    edge_copy.wait()

    def first_layer(i, carry):
        first = pl.multiple_of(i * block, block)
        for j in range(block):
            picked[1, pl.ds(j * parts, parts), :] = table[receiver[first + j]]
        rows = jnp.concatenate([picked[1, pl.ds(k, block, stride=parts), :] for k in range(parts)], axis=1)
        pre_buf[pl.ds(first, block), :] = dot(edge_buf[pl.ds(first, block), :], inner[:width, :]) + rows + bias[...]
        return carry

    lax.fori_loop(0, edges // block, first_layer, 0)
    pre_copy = pltpu.make_async_copy(pre_buf, pre_hbm, pre_sem)
    pre_copy.start()
    pre_copy.wait()
    for copy in near_copies:
        copy.wait()
    pltpu.make_async_copy(
        far_out.at[pl.ds(0, peers - 1)], far_out.at[pl.ds(0, peers - 1)], far_recv_sem
    ).wait()
    pltpu.make_async_copy(
        far_buf.at[pl.ds(0, peers - 1)], far_buf.at[pl.ds(0, peers - 1)], far_send_sem
    ).wait()


def exchange(n_row, n_col, far_send, near_send, receiver, node_lat, edge_lat, inner, bias):
    nodes, width = node_lat.shape
    edges = edge_lat.shape[0]
    peers, slots = far_send.shape[1:]
    halo = near_send.shape[2]
    parts = width // LANES
    block = min(512, edges)
    smem = pl.BlockSpec(memory_space=pltpu.SMEM)
    vmem = pl.BlockSpec(memory_space=pltpu.VMEM)
    hbm = pl.BlockSpec(memory_space=pl.ANY)
    return pl.pallas_call(
        functools.partial(exchange_kernel, n_row, n_col, block),
        out_shape=(
            jax.ShapeDtypeStruct((edges, width), F32),
            jax.ShapeDtypeStruct((peers, slots, width), BF16),
            jax.ShapeDtypeStruct((2, halo, width), BF16),
        ),
        in_specs=[smem, smem, smem, vmem, hbm, vmem, vmem],
        out_specs=(hbm, hbm, hbm),
        scratch_shapes=[
            pltpu.VMEM((nodes, parts, LANES), F32),
            pltpu.VMEM((nodes, parts, LANES), F32),
            pltpu.VMEM((2, block * parts, LANES), F32),
            pltpu.VMEM((peers, slots, width), BF16),
            pltpu.VMEM((2, halo, width), BF16),
            pltpu.VMEM((edges, width), BF16),
            pltpu.VMEM((edges, width), F32),
            pltpu.SemaphoreType.DMA,
            pltpu.SemaphoreType.DMA,
            pltpu.SemaphoreType.DMA((2,)),
            pltpu.SemaphoreType.DMA((2,)),
            pltpu.SemaphoreType.DMA,
            pltpu.SemaphoreType.DMA,
        ],
        compiler_params=pltpu.CompilerParams(
            collective_id=0, has_side_effects=True, vmem_limit_bytes=40 << 20
        ),
        name="exchange",
    )(far_send, near_send, receiver, node_lat, edge_lat, inner, bias)


def update_kernel(
    sender, receiver, pre, edge, node, near, far, inner, edge_outer, edge_offset, edge_gain, edge_shift,
    node_inner, node_bias, node_outer, node_offset, node_gain, node_shift,
    edge_new, node_new, table, picked, incoming,
):
    step, steps = pl.program_id(0), pl.num_programs(0)
    block, width = edge.shape
    nodes = node.shape[0]
    parts = width // LANES

    @pl.when(step == 0)
    def _():
        first = 0
        for source in (node, near, far):
            for c in range(0, source.shape[0], LANES):
                put_rows(table, first, dot(source[c : c + LANES, :], inner[...]))
                first += LANES
        incoming[...] = jnp.zeros_like(incoming)

    base = step * block
    for j in range(block):
        start = pl.multiple_of(sender[base + j] * parts, parts)
        picked[pl.ds(j * parts, parts), :] = table[pl.ds(start, parts), :]
    rows = jnp.concatenate([picked[pl.ds(k, block, stride=parts), :] for k in range(parts)], axis=1)
    hidden = silu(pre[...] + rows).astype(BF16)
    post = dot(hidden, edge_outer[...]) + edge_offset[...]
    message = layer_norm(post, edge_gain[...], edge_shift[...]).astype(BF16)
    edge_new[...] = (edge[...].astype(F32) + message.astype(F32)).astype(BF16)
    node_ids = lax.broadcasted_iota(jnp.int32, (nodes, block), 0)
    hot = (node_ids == receiver[...].reshape(1, block)).astype(F32).astype(BF16)
    incoming[...] += dot(hot, message)

    @pl.when(step == steps - 1)
    def _():
        total = incoming[...].astype(BF16)
        node_pre = dot(node[...], node_inner[:width, :]) + dot(total, node_inner[width:, :]) + node_bias[...]
        node_post = dot(silu(node_pre).astype(BF16), node_outer[...]) + node_offset[...]
        node_new[...] = (
            node[...].astype(F32) + layer_norm(node_post, node_gain[...], node_shift[...])
        ).astype(BF16)


def update(sender, receiver, pre, edge_lat, node_lat, near, far, inner, edge_outer, node_inner, node_outer, vectors):
    edges, width = edge_lat.shape
    nodes = node_lat.shape[0]
    table_rows = nodes + near.shape[0] + far.shape[0]
    parts = width // LANES
    block = min(512, edges)
    steps = edges // block
    once = pl.Buffered(1)

    def whole(array):
        return pl.BlockSpec(array.shape, lambda i, ids: (0,) * array.ndim, pipeline_mode=once)

    rows = pl.BlockSpec((block, width), lambda i, ids: (i, 0))
    row_ids = pl.BlockSpec((1, 1, block), lambda i, ids: (i, 0, 0))
    sender_part = pl.BlockSpec((width, width), lambda i, ids: (1, 0), pipeline_mode=once)
    edge_offset, edge_gain, edge_shift, node_bias, node_offset, node_gain, node_shift = vectors
    arrays = (
        receiver.reshape(steps, 1, block), pre, edge_lat, node_lat, near, far, inner,
        edge_outer, edge_offset, edge_gain, edge_shift,
        node_inner, node_bias, node_outer, node_offset, node_gain, node_shift,
    )
    return pl.pallas_call(
        update_kernel,
        grid_spec=pltpu.PrefetchScalarGridSpec(
            num_scalar_prefetch=1,
            grid=(steps,),
            in_specs=[row_ids, rows, rows, whole(node_lat), whole(near), whole(far), sender_part]
            + [whole(array) for array in arrays[7:]],
            out_specs=[rows, pl.BlockSpec((nodes, width), lambda i, ids: (0, 0))],
            scratch_shapes=[
                pltpu.VMEM((table_rows * parts, LANES), F32),
                pltpu.VMEM((block * parts, LANES), F32),
                pltpu.VMEM((nodes, width), F32),
            ],
        ),
        out_shape=[
            jax.ShapeDtypeStruct((edges, width), BF16),
            jax.ShapeDtypeStruct((nodes, width), BF16),
        ],
        compiler_params=pltpu.CompilerParams(vmem_limit_bytes=40 << 20),
        name="update",
    )(sender, *arrays)


def solution(mesh):
    n_row, n_col = mesh.shape["row"], mesh.shape["col"]

    def shards(
        node_lat, edge_lat, near_send, far_send, edge_sender, edge_receiver,
        edge_inner, edge_bias, edge_outer, edge_offset, edge_gain, edge_shift,
        node_inner, node_bias, node_outer, node_offset, node_gain, node_shift,
    ):
        width = node_lat.shape[1]
        vectors = [
            v.reshape(1, -1)
            for v in (edge_offset, edge_gain, edge_shift, node_bias, node_offset, node_gain, node_shift)
        ]
        pre, far, near = exchange(
            n_row, n_col, far_send, near_send, edge_receiver, node_lat, edge_lat,
            edge_inner, edge_bias.reshape(1, -1),
        )
        edge_new, node_new = update(
            edge_sender, edge_receiver, pre, edge_lat, node_lat,
            near.reshape(-1, width), far.reshape(-1, width),
            edge_inner, edge_outer, node_inner, node_outer, vectors,
        )
        return edge_new, node_new

    whole = P()
    split = P(("row", "col"))
    return jax.shard_map(
        shards, mesh=mesh, in_specs=(split,) * 6 + (whole,) * 12, out_specs=(split, split), check_vma=False
    )
```

time: 176 us -> 59.8 us (0.34)
  matrix products: 92.2 us -> 0 us
  Pallas kernels: 0 us -> 48.7 us
  local copies, waits for them, and re-layouts: 36 us -> 9.85 us
  other arithmetic: 16.7 us -> 0 us
  starting transfers between devices: 16.4 us -> 0 us
  waiting for transfers between devices: 11.6 us -> 0 us
    dot_general x33 -> x0, matrix products: 92.2 us -> none  [the longest x8 28.5 us: one_block(): jnp.dot(sender_hot, lookup_table, preferred_element_type=jnp.float32)]
    pallas_call x0 -> x2, Pallas kernels: none -> 48.7 us  [the longest x1 29.7 us: exchange(): pl.pallas_call(functools.partial(exchange_kernel, n_row, n_col, block), o...]
    dynamic_update_slice x16 -> x0, local copies, waits for them, and re-layouts: 16.7 us -> none  [shards(): lax.scan(one_block, start_sum, (edge_blocks, sender_blocks, receiver_bloc...]
    all_to_all x1 -> x0, starting transfers between devices: 11.5 us -> none  [shards(): lax.all_to_all(far_rows, ('row', 'col'), split_axis=0, concat_axis=0, til...]
    dynamic_slice x24 -> x0, local copies, waits for them, and re-layouts: 10.4 us -> none  [shards(): lax.scan(one_block, start_sum, (edge_blocks, sender_blocks, receiver_bloc...]
    ppermute x2 -> x0, waiting for transfers between devices: 9.96 us -> none  [from_behind(): lax.ppermute(shard, axis, [(i, (i + by) % devices) for i in range(devices)])]
    broadcast_in_dim x9 -> x0, other arithmetic: 8.65 us -> none  [shards(): lax.scan(one_block, start_sum, (edge_blocks, sender_blocks, receiver_bloc...]
    unnamed x30 -> x39, local copies, waits for them, and re-layouts: 2.1 us -> 9.85 us
  transfers between devices with their start and end apart: 3 -> 0, of which waited for: 3 -> 0; matrix products, arithmetic and copies ran while one was open for 1% -> 0% of each run, Pallas kernels for 0% -> 0%
where the time goes in v1:
time: 59.8 us; the launch traced here: 59.4 us
  Pallas kernels  48.7 us (81%)
  local copies, waits for them, and re-layouts  9.85 us (16%)
  between operations  0.81 us (1%)
    pallas_call x1, Pallas kernels, exchange(): pl.pallas_call(functools.partial(exchange_kernel, n_row, n_col, block), o...  29.7 us
    pallas_call x1, Pallas kernels, update(): pl.pallas_call(update_kernel, grid_spec=pltpu.PrefetchScalarGridSpec(num_...  19 us
    unnamed x39, local copies, waits for them, and re-layouts  9.85 us

profile of v1, /device:TPU:1, one launch (start us, length us, event | category | flops | bytes accessed | tf_op | source)
XLA Modules:
  0.0 59.4 jit_solution(17599102565750518590)
XLA Ops:
  0.6 0.0 copy-start.17
  0.6 0.0 copy-start.16
  0.7 0.0 copy-start.15
  0.7 0.0 copy-start.14
  0.7 0.0 copy-start.13
  0.7 0.0 copy-start.12
  0.7 0.0 copy-start.11
  0.7 0.0 copy-start.9
  0.7 0.8 %copy.20.far_ids = s32[1,128,8]{2,1,0:T(8,128)S(1)} copy(s32[1,128,8]{1,2,0:T(8,128)} %param.21) | data formatting | bytes 8192 | tf_op args[3]
  1.5 0.0 copy-start
  1.6 2.2 %copy-done = bf16[4096,512]{1,0:T(8,128)(2,1)S(1)} copy-done((bf16[4096,512]{1,0:T(8,128)(2,1)S(1)}, bf16[4096,512]{1,0:T(8,128)(2,1)}, u32[]{:S(2)}) %copy-start) | copy-done | bytes 4194328
  3.7 0.0 copy-start.2
  3.7 1.4 %copy-done.2 = bf16[1536,512]{1,0:T(8,128)(2,1)S(1)} copy-done((bf16[1536,512]{1,0:T(8,128)(2,1)S(1)}, bf16[1536,512]{1,0:T(8,128)(2,1)}, u32[]{:S(2)}) %copy-start.2) | copy-done | bytes 1572888
  5.1 0.0 copy-start.4
  5.1 1.0 %copy-done.4 = bf16[512,512]{1,0:T(8,128)(2,1)S(1)} copy-done((bf16[512,512]{1,0:T(8,128)(2,1)S(1)}, bf16[512,512]{1,0:T(8,128)(2,1)}, u32[]{:S(2)}) %copy-start.4) | copy-done | bytes 524312
  6.2 0.0 copy-start.8
  6.2 0.7 %copy-done.8 = s32[4096]{0:T(1024)S(1)} copy-done((s32[4096]{0:T(1024)S(1)}, s32[4096]{0:T(1024)}, u32[]{:S(2)}) %copy-start.8) | copy-done | bytes 16408
  6.9 0.0 copy-start.10
  6.9 0.7 %copy-done.10 = f32[512]{0:T(512)S(1)} copy-done((f32[512]{0:T(512)S(1)}, f32[512]{0:T(512)}, u32[]{:S(2)}) %copy-start.10) | copy-done | bytes 2072
  7.6 0.0 copy-start.18
  7.6 0.7 %copy-done.18 = s32[1,2,64]{2,1,0:T(2,128)S(1)} copy-done((s32[1,2,64]{2,1,0:T(2,128)S(1)}, s32[1,2,64]{2,1,0:T(2,128)}, u32[]{:S(2)}) %copy-start.18) | copy-done | bytes 536
  8.3 0.0 copy-start.1
  8.3 0.0 copy-start.3
  8.3 0.0 copy-start.6
  8.3 29.7 %exchange.1 = (f32[4096,512]{1,0:T(8,128)}, bf16[128,8,512]{2,1,0:T(8,128)(2,1)S(1)}, bf16[2,64,512]{2,1,0:T(8,128)(2,1)S(1)}) custom-call(s32[1,128,8]{2,1,0:T(8,128)S(1)} %copy.20.far_ids, s32[1,2,64]{2,1,0:T(2,128)S(1)} %copy-done.18, s32[4096]{0:T(1024)S(1)} %copy-done.8, bf16[512,512]{1,0:T(8,128)(2,1)S(1)} %copy-done.4, bf16[4096,512]{1,0:T(8,128)(2,1)S(1)} %copy-done, ...), custom_call_target="tpu_custom_call" | custom-call | tf_op jit(solution)/shard_map/exchange/pallas_call | solution.py:158
  38.0 0.0 copy-done.17
  38.0 0.0 copy-done.16
  38.0 0.0 copy-done.15
  38.0 0.0 copy-done.14
  38.0 0.0 copy-done.13
  38.0 0.0 copy-done.12
  38.0 0.0 copy-done.11
  38.0 0.0 copy-done.9
  38.0 0.0 copy-done.1
  38.1 0.0 copy-done.3
  38.1 0.0 copy-done.6
  38.1 0.0 copy-start.5
  38.1 1.2 %copy-done.5 = bf16[1024,512]{1,0:T(8,128)(2,1)S(1)} copy-done((bf16[1024,512]{1,0:T(8,128)(2,1)S(1)}, bf16[1024,512]{1,0:T(8,128)(2,1)}, u32[]{:S(2)}) %copy-start.5) | copy-done | bytes 1048600
  39.3 0.0 copy-start.7
  39.3 1.0 %copy-done.7 = bf16[512,512]{1,0:T(8,128)(2,1)S(1)} copy-done((bf16[512,512]{1,0:T(8,128)(2,1)S(1)}, bf16[512,512]{1,0:T(8,128)(2,1)}, u32[]{:S(2)}) %copy-start.7) | copy-done | bytes 524312
  40.3 19.0 %update.1 = (bf16[4096,512]{1,0:T(8,128)(2,1)}, bf16[512,512]{1,0:T(8,128)(2,1)}) custom-call(s32[4096]{0:T(1024)S(1)} %copy-done.9, s32[8,1,512]{2,1,0:T(1,128)S(1)} %bitcast.13, f32[4096,512]{1,0:T(8,128)} %get-tuple-element.5.pre, bf16[4096,512]{1,0:T(8,128)(2,1)S(1)} %copy-done.1, bf16[512,512]{1,0:T(8,128)(2,1)S(1)} %copy-done.4, ...), custom_call_target="tpu_custom_call" | custom-call | tf_op jit(solution)/shard_map/update/pallas_call | solution.py:252
Async XLA Ops:
  0.6 37.3 %copy-start.17 = (f32[512]{0:T(512)S(1)}, f32[512]{0:T(512)}, u32[]{:S(2)}) copy-start(f32[512]{0:T(512)} %param.35) | copy-start | bytes 6148
  0.6 37.3 %copy-start.16 = (f32[512]{0:T(512)S(1)}, f32[512]{0:T(512)}, u32[]{:S(2)}) copy-start(f32[512]{0:T(512)} %param.34) | copy-start | bytes 6148
  0.7 37.3 %copy-start.15 = (f32[512]{0:T(512)S(1)}, f32[512]{0:T(512)}, u32[]{:S(2)}) copy-start(f32[512]{0:T(512)} %param.33) | copy-start | bytes 6148
  0.7 37.3 %copy-start.14 = (f32[512]{0:T(512)S(1)}, f32[512]{0:T(512)}, u32[]{:S(2)}) copy-start(f32[512]{0:T(512)} %param.31) | copy-start | bytes 6148
  0.7 37.3 %copy-start.13 = (f32[512]{0:T(512)S(1)}, f32[512]{0:T(512)}, u32[]{:S(2)}) copy-start(f32[512]{0:T(512)} %param.29) | copy-start | bytes 6148
  0.7 37.3 %copy-start.12 = (f32[512]{0:T(512)S(1)}, f32[512]{0:T(512)}, u32[]{:S(2)}) copy-start(f32[512]{0:T(512)} %param.28) | copy-start | bytes 6148
  0.7 37.3 %copy-start.11 = (f32[512]{0:T(512)S(1)}, f32[512]{0:T(512)}, u32[]{:S(2)}) copy-start(f32[512]{0:T(512)} %param.27) | copy-start | bytes 6148
  0.7 37.3 %copy-start.9 = (s32[4096]{0:T(1024)S(1)}, s32[4096]{0:T(1024)}, u32[]{:S(2)}) copy-start(s32[4096]{0:T(1024)} %sender.1) | copy-start | bytes 49156
  1.5 2.2 %copy-start = (bf16[4096,512]{1,0:T(8,128)(2,1)S(1)}, bf16[4096,512]{1,0:T(8,128)(2,1)}, u32[]{:S(2)}) copy-start(bf16[4096,512]{1,0:T(8,128)(2,1)} %edge.1) | copy-start | bytes 12582916
  3.7 1.4 %copy-start.2 = (bf16[1536,512]{1,0:T(8,128)(2,1)S(1)}, bf16[1536,512]{1,0:T(8,128)(2,1)}, u32[]{:S(2)}) copy-start(bf16[1536,512]{1,0:T(8,128)(2,1)} %inner.3) | copy-start | bytes 4718596
  5.1 1.0 %copy-start.4 = (bf16[512,512]{1,0:T(8,128)(2,1)S(1)}, bf16[512,512]{1,0:T(8,128)(2,1)}, u32[]{:S(2)}) copy-start(bf16[512,512]{1,0:T(8,128)(2,1)} %node.3) | copy-start | bytes 1572868
  6.2 0.7 %copy-start.8 = (s32[4096]{0:T(1024)S(1)}, s32[4096]{0:T(1024)}, u32[]{:S(2)}) copy-start(s32[4096]{0:T(1024)} %receiver.1) | copy-start | bytes 49156
  6.9 0.7 %copy-start.10 = (f32[512]{0:T(512)S(1)}, f32[512]{0:T(512)}, u32[]{:S(2)}) copy-start(f32[512]{0:T(512)} %param.25) | copy-start | bytes 6148
  7.6 0.7 %copy-start.18 = (s32[1,2,64]{2,1,0:T(2,128)S(1)}, s32[1,2,64]{2,1,0:T(2,128)}, u32[]{:S(2)}) copy-start(s32[1,2,64]{2,1,0:T(2,128)} %near_ids.1) | copy-start | bytes 1540
  8.3 29.8 %copy-start.1 = (bf16[4096,512]{1,0:T(8,128)(2,1)S(1)}, bf16[4096,512]{1,0:T(8,128)(2,1)}, u32[]{:S(2)}) copy-start(bf16[4096,512]{1,0:T(8,128)(2,1)} %edge.1) | copy-start | bytes 12582916
  8.3 29.8 %copy-start.3 = (bf16[1536,512]{1,0:T(8,128)(2,1)S(1)}, bf16[1536,512]{1,0:T(8,128)(2,1)}, u32[]{:S(2)}) copy-start(bf16[1536,512]{1,0:T(8,128)(2,1)} %inner.3) | copy-start | bytes 4718596
  8.3 29.8 %copy-start.6 = (bf16[512,512]{1,0:T(8,128)(2,1)S(1)}, bf16[512,512]{1,0:T(8,128)(2,1)}, u32[]{:S(2)}) copy-start(bf16[512,512]{1,0:T(8,128)(2,1)} %edge_outer.1) | copy-start | bytes 1572868
  38.1 1.2 %copy-start.5 = (bf16[1024,512]{1,0:T(8,128)(2,1)S(1)}, bf16[1024,512]{1,0:T(8,128)(2,1)}, u32[]{:S(2)}) copy-start(bf16[1024,512]{1,0:T(8,128)(2,1)} %node_inner.1) | copy-start | bytes 3145732
  39.3 1.0 %copy-start.7 = (bf16[512,512]{1,0:T(8,128)(2,1)S(1)}, bf16[512,512]{1,0:T(8,128)(2,1)}, u32[]{:S(2)}) copy-start(bf16[512,512]{1,0:T(8,128)(2,1)} %node_outer.1) | copy-start | bytes 1572868

commit v2 on v1

--- a/solution.py
+++ b/solution.py
@@ -11,6 +11,7 @@
 BF16 = jnp.bfloat16
 MESH = pl.DeviceIdType.MESH
 LANES = 128
+VMEM_BYTES = 60 * 1024 * 1024
 
 
 def dot(a, b):
@@ -87,7 +88,7 @@
     lax.fori_loop(0, halo // 16, pick_near, 0)
 
     def pick_far(p, carry):
-        ids = [jnp.maximum(far_ids[0, p, j], 0) for j in range(slots)]
+        ids = [jnp.maximum(far_ids[0, j, p], 0) for j in range(slots)]
         for k, values in enumerate(pick(ids)):
             far_buf[p, :, k * LANES : (k + 1) * LANES] = values
         return carry
@@ -148,7 +149,7 @@
 def exchange(n_row, n_col, far_send, near_send, receiver, node_lat, edge_lat, inner, bias):
     nodes, width = node_lat.shape
     edges = edge_lat.shape[0]
-    peers, slots = far_send.shape[1:]
+    slots, peers = far_send.shape[1:]
     halo = near_send.shape[2]
     parts = width // LANES
     block = min(512, edges)
@@ -180,7 +181,7 @@
             pltpu.SemaphoreType.DMA,
         ],
         compiler_params=pltpu.CompilerParams(
-            collective_id=0, has_side_effects=True, vmem_limit_bytes=40 << 20
+            collective_id=0, has_side_effects=True, vmem_limit_bytes=VMEM_BYTES
         ),
         name="exchange",
     )(far_send, near_send, receiver, node_lat, edge_lat, inner, bias)
@@ -267,7 +268,7 @@
             jax.ShapeDtypeStruct((edges, width), BF16),
             jax.ShapeDtypeStruct((nodes, width), BF16),
         ],
-        compiler_params=pltpu.CompilerParams(vmem_limit_bytes=40 << 20),
+        compiler_params=pltpu.CompilerParams(vmem_limit_bytes=VMEM_BYTES),
         name="update",
     )(sender, *arrays)
 
@@ -286,7 +287,7 @@
             for v in (edge_offset, edge_gain, edge_shift, node_bias, node_offset, node_gain, node_shift)
         ]
         pre, far, near = exchange(
-            n_row, n_col, far_send, near_send, edge_receiver, node_lat, edge_lat,
+            n_row, n_col, far_send.swapaxes(1, 2), near_send, edge_receiver, node_lat, edge_lat,
             edge_inner, edge_bias.reshape(1, -1),
         )
         edge_new, node_new = update(

time: 59.8 us -> 51.2 us (0.86)
  local copies, waits for them, and re-layouts: 9.85 us -> 0 us
  Pallas kernels: 48.7 us -> 50.4 us
    unnamed x39 -> x0, local copies, waits for them, and re-layouts: 9.85 us -> none
    pallas_call x1, Pallas kernels: 19 us -> 21.2 us  [update(): pl.pallas_call(update_kernel, grid_spec=pltpu.PrefetchScalarGridSpec(num_...]
where the time goes in v2:
time: 51.2 us; the launch traced here: 51 us
  Pallas kernels  50.4 us (98%)
  between operations  0.64 us (1%)
    pallas_call x1, Pallas kernels, exchange(): pl.pallas_call(functools.partial(exchange_kernel, n_row, n_col, block), o...  29.2 us
    pallas_call x1, Pallas kernels, update(): pl.pallas_call(update_kernel, grid_spec=pltpu.PrefetchScalarGridSpec(num_...  21.2 us

profile of v2, /device:TPU:1, one launch (start us, length us, event | category | flops | bytes accessed | tf_op | source)
XLA Modules:
  0.0 51.0 jit_solution(10628403007277162254)
XLA Ops:
  0.6 29.2 %exchange.1 = (f32[4096,512]{1,0:T(8,128)}, bf16[128,8,512]{2,1,0:T(8,128)(2,1)}, bf16[2,64,512]{2,1,0:T(8,128)(2,1)}) custom-call(s32[1,8,128]{2,1,0:T(8,128)} %bitcast.15, s32[1,2,64]{2,1,0:T(2,128)} %near_ids.1, s32[4096]{0:T(1024)} %receiver.1, bf16[512,512]{1,0:T(8,128)(2,1)} %node.3, bf16[4096,512]{1,0:T(8,128)(2,1)} %edge.1, bf16[1536,512]{1,0:T(8,128)(2,1)} %inner.3, ...), custom_call_target="tpu_custom_call" | custom-call | tf_op jit(solution)/shard_map/exchange/pallas_call | solution.py:159
  29.9 21.2 %update.1 = (bf16[4096,512]{1,0:T(8,128)(2,1)}, bf16[512,512]{1,0:T(8,128)(2,1)}) custom-call(s32[4096]{0:T(1024)} %sender.1, s32[8,1,512]{2,1,0:T(1,128)} %bitcast.14, f32[4096,512]{1,0:T(8,128)} %get-tuple-element.5.pre, bf16[4096,512]{1,0:T(8,128)(2,1)} %edge.1, bf16[512,512]{1,0:T(8,128)(2,1)} %node.3, bf16[128,512]{1,0:T(8,128)(2,1)} %bitcast.13, ...), custom_call_target="tpu_custom_call" | custom-call | tf_op jit(solution)/shard_map/update/pallas_call | solution.py:253

commit v3 on v2

v3 whole, which is shorter than its diff:
```python
import functools

import jax
import jax.numpy as jnp
from jax import lax
from jax.experimental import pallas as pl
from jax.experimental.pallas import tpu as pltpu
from jax.sharding import PartitionSpec as P

F32 = jnp.float32
BF16 = jnp.bfloat16
MESH = pl.DeviceIdType.MESH
LANES = 128
PIECE = 64
UNROLL = 8
VMEM_BYTES = 60 * 1024 * 1024


def dot(a, b):
    return jnp.dot(a, b, preferred_element_type=F32)


def half_silu(half):
    return half * jnp.tanh(half) + half


def layer_norm(values, gain, shift):
    centre = jnp.mean(values, axis=-1, keepdims=True)
    off = values - centre
    spread = jnp.mean(off * off, axis=-1, keepdims=True)
    return off * lax.rsqrt(spread + 1e-05) * gain + shift


def put_rows(dst, first, values):
    rows, width = values.shape
    parts = width // LANES
    for k in range(parts):
        dst[pl.ds(first * parts + k, rows, stride=parts), :] = values[:, k * LANES : (k + 1) * LANES]


def exchange_kernel(
    n_row, n_col, block,
    far_ids, near_ids, receiver, sender, node, edge_hbm, inner_hbm, bias, node_inner_hbm, node_bias,
    pre_hbm, far_out, table_out, node_out, sender_out,
    node_parts, table, near_table, picked, rows_buf, far_buf, near_buf, near_in, edge_buf, pre_buf, inner, node_inner,
    far_send_sem, far_recv_sem, near_send_sem, near_recv_sem, load_sem, pre_sem, out_sem,
):
    peers = n_row * n_col
    row, col = lax.axis_index("row"), lax.axis_index("col")
    me = row * n_col + col
    nodes, width = node.shape
    edges = edge_hbm.shape[0]
    parts = width // LANES
    slots = far_buf.shape[1]
    halo = near_buf.shape[1]

    barrier = pltpu.get_barrier_semaphore()

    def place(i):
        other = lax.rem(me + i, peers)
        return other, (lax.div(other, n_col), lax.rem(other, n_col))

    def for_peers(visit):
        for i in range(1, UNROLL):
            visit(i)

        def some(q, carry):
            for i in range(UNROLL):
                visit(q * UNROLL + i)
            return carry

        lax.fori_loop(1, peers // UNROLL, some, 0)

    def greet(i):
        pl.semaphore_signal(barrier, inc=1, device_id=place(i)[1], device_id_type=MESH)

    for_peers(greet)
    loads = [
        pltpu.make_async_copy(inner_hbm, inner, load_sem.at[0]),
        pltpu.make_async_copy(edge_hbm, edge_buf, load_sem.at[1]),
        pltpu.make_async_copy(node_inner_hbm.at[pl.ds(0, width)], node_inner, load_sem.at[2]),
    ]
    for load in loads:
        load.start()

    put_rows(node_parts, 0, node[...].astype(F32))
    node_rows = node_parts.reshape(nodes, parts, LANES)

    def pick(at, ids):
        for j, row_id in enumerate(ids):
            picked[at, pl.ds(j * parts, parts), :] = node_rows[row_id]
        return [picked[at, pl.ds(k, len(ids), stride=parts), :].astype(BF16) for k in range(parts)]

    def pick_near(i, carry):
        for side in range(2):
            first = pl.multiple_of(i * 16, 16)
            for k, values in enumerate(pick(side, [near_ids[0, side, first + j] for j in range(16)])):
                near_buf[side, pl.ds(first, 16), k * LANES : (k + 1) * LANES] = values
        return carry

    lax.fori_loop(0, halo // 16, pick_near, 0)

    def pick_far(q, carry):
        for i in range(picked.shape[0]):
            p = q * picked.shape[0] + i
            ids = [jnp.maximum(far_ids[0, j, p], 0) for j in range(slots)]
            for k, values in enumerate(pick(i, ids)):
                far_buf[p, :, k * LANES : (k + 1) * LANES] = values
        return carry

    lax.fori_loop(0, peers // picked.shape[0], pick_far, 0)

    pl.semaphore_wait(barrier, peers - 1)

    east = (row, lax.rem(col + 1, n_col))
    west = (row, lax.rem(col + n_col - 1, n_col))
    near_copies = [
        pltpu.make_async_remote_copy(
            src_ref=near_buf.at[side], dst_ref=near_in.at[side],
            send_sem=near_send_sem.at[side], recv_sem=near_recv_sem.at[side],
            device_id=target, device_id_type=MESH,
        )
        for side, target in enumerate((east, west))
    ]
    for copy in near_copies:
        copy.start()

    def send(i):
        other, target = place(i)
        pltpu.make_async_remote_copy(
            src_ref=far_buf.at[other], dst_ref=far_out.at[me],
            send_sem=far_send_sem, recv_sem=far_recv_sem,
            device_id=target, device_id_type=MESH,
        ).start()

    for_peers(send)

    sender_out[...] = sender[...] * parts
    loads[0].wait()
    put_rows(table, 0, dot(node[...], inner[2 * width :, :]))
    table_rows = table.reshape(nodes, parts, LANES)
    loads[1].wait()

    def pre_copy(first):
        return pltpu.make_async_copy(pre_buf.at[pl.ds(first, block)], pre_hbm.at[pl.ds(first, block)], pre_sem)

    def first_layer(i, carry):
        first = pl.multiple_of(i * block, block)
        for j in range(block):
            rows_buf[pl.ds(j * parts, parts), :] = table_rows[receiver[first + j]]
        rows = jnp.concatenate([rows_buf[pl.ds(k, block, stride=parts), :] for k in range(parts)], axis=1)
        total = dot(edge_buf[pl.ds(first, block), :], inner[:width, :]) + rows + bias[...]
        pre_buf[pl.ds(first, block), :] = 0.5 * total
        pre_copy(first).start()
        return carry

    lax.fori_loop(0, edges // block, first_layer, 0)

    for first in range(0, nodes, LANES):
        values = dot(node[first : first + LANES, :], inner[width : 2 * width, :])
        put_rows(near_table, first, 0.5 * values)
    loads[2].wait()
    node_out[...] = 0.5 * (dot(node[...], node_inner[...]) + node_bias[...])
    for side, copy in enumerate(near_copies):
        copy.wait()
        values = dot(near_in[side], inner[width : 2 * width, :])
        put_rows(near_table, nodes + side * halo, 0.5 * values)
    table_copy = pltpu.make_async_copy(near_table, table_out, out_sem)
    table_copy.start()

    pltpu.make_async_copy(pre_buf, pre_hbm, pre_sem).wait()
    table_copy.wait()
    pltpu.make_async_copy(
        far_out.at[pl.ds(0, peers - 1)], far_out.at[pl.ds(0, peers - 1)], far_recv_sem
    ).wait()
    pltpu.make_async_copy(
        far_buf.at[pl.ds(0, peers - 1)], far_buf.at[pl.ds(0, peers - 1)], far_send_sem
    ).wait()


def exchange(
    n_row, n_col, far_send, near_send, receiver, sender, node_lat, edge_lat, inner, bias, node_inner, node_bias
):
    nodes, width = node_lat.shape
    edges = edge_lat.shape[0]
    slots, peers = far_send.shape[1:]
    halo = near_send.shape[2]
    parts = width // LANES
    block = min(512, edges)
    smem = pl.BlockSpec(memory_space=pltpu.SMEM)
    vmem = pl.BlockSpec(memory_space=pltpu.VMEM)
    hbm = pl.BlockSpec(memory_space=pl.ANY)
    return pl.pallas_call(
        functools.partial(exchange_kernel, n_row, n_col, block),
        out_shape=(
            jax.ShapeDtypeStruct((edges, width), F32),
            jax.ShapeDtypeStruct((peers, slots, width), BF16),
            jax.ShapeDtypeStruct(((nodes + 2 * halo) * parts, LANES), F32),
            jax.ShapeDtypeStruct((nodes, width), F32),
            jax.ShapeDtypeStruct(sender.shape, jnp.int32),
        ),
        in_specs=[smem, smem, smem, vmem, vmem, hbm, hbm, vmem, hbm, vmem],
        out_specs=(hbm, hbm, hbm, vmem, vmem),
        scratch_shapes=[
            pltpu.VMEM((nodes * parts, LANES), F32),
            pltpu.VMEM((nodes * parts, LANES), F32),
            pltpu.VMEM(((nodes + 2 * halo) * parts, LANES), F32),
            pltpu.VMEM((4, 16 * parts, LANES), F32),
            pltpu.VMEM((block * parts, LANES), F32),
            pltpu.VMEM((peers, slots, width), BF16),
            pltpu.VMEM((2, halo, width), BF16),
            pltpu.VMEM((2, halo, width), BF16),
            pltpu.VMEM((edges, width), BF16),
            pltpu.VMEM((edges, width), F32),
            pltpu.VMEM(inner.shape, BF16),
            pltpu.VMEM((width, width), BF16),
            pltpu.SemaphoreType.DMA,
            pltpu.SemaphoreType.DMA,
            pltpu.SemaphoreType.DMA((2,)),
            pltpu.SemaphoreType.DMA((2,)),
            pltpu.SemaphoreType.DMA((3,)),
            pltpu.SemaphoreType.DMA,
            pltpu.SemaphoreType.DMA,
        ],
        compiler_params=pltpu.CompilerParams(
            collective_id=0, has_side_effects=True, vmem_limit_bytes=VMEM_BYTES
        ),
        name="exchange",
    )(far_send, near_send, receiver, sender, node_lat, edge_lat, inner, bias, node_inner, node_bias)


def update_kernel(
    sender, receiver, pre, edge, far, inner, edge_outer, edge_offset, edge_gain, edge_shift,
    table_hbm, node_hbm, node_part_hbm, node_inner_hbm, node_outer_hbm, node_offset, node_gain, node_shift,
    edge_new, node_new,
    table, incoming, hidden, post, message, rows_a, rows_b, node, node_part, node_inner, node_outer, load_sem,
):
    step, steps = pl.program_id(0), pl.num_programs(0)
    block, width = edge.shape
    nodes = node.shape[0]
    parts = width // LANES
    unit = rows_a.shape[0] // parts
    units = block // unit
    rows = (rows_a, rows_b)
    near_rows = table_hbm.shape[0]

    table_load = pltpu.make_async_copy(table_hbm, table.at[pl.ds(0, near_rows)], load_sem.at[0])
    node_loads = [
        pltpu.make_async_copy(node_inner_hbm.at[pl.ds(width, width)], node_inner, load_sem.at[1]),
        pltpu.make_async_copy(node_outer_hbm, node_outer, load_sem.at[2]),
        pltpu.make_async_copy(node_hbm, node, load_sem.at[3]),
        pltpu.make_async_copy(node_part_hbm, node_part, load_sem.at[4]),
    ]

    def gather(first, buffer, piece):
        for j in range(piece, piece + PIECE):
            start = pl.multiple_of(sender[first + j], parts)
            buffer[pl.ds(j * parts, parts), :] = table[pl.ds(start, parts), :]

    def activate(u, piece):
        at = u * unit + piece
        for k in range(parts):
            lanes = slice(k * LANES, (k + 1) * LANES)
            near = rows[u % 2][pl.ds(piece * parts + k, PIECE, stride=parts), :]
            hidden[at : at + PIECE, lanes] = half_silu(pre[at : at + PIECE, lanes] + near).astype(BF16)

    def finish(u, piece):
        at = u * unit + piece
        values = layer_norm(post[at : at + PIECE, :] + edge_offset[...], edge_gain[...], edge_shift[...]).astype(BF16)
        message[at : at + PIECE, :] = values
        edge_new[at : at + PIECE, :] = edge[at : at + PIECE, :] + values

    def scatter(u):
        ids = receiver[0, :, u * unit : (u + 1) * unit].astype(jnp.int16)
        node_ids = lax.broadcasted_iota(jnp.int16, (nodes, unit), 0)
        hot = jnp.where(node_ids == ids, jnp.bfloat16(1), jnp.bfloat16(0))
        incoming[...] += dot(hot, message[u * unit : (u + 1) * unit, :])

    @pl.when(step == 0)
    def _():
        table_load.start()
        for load in node_loads:
            load.start()
        for first in range(0, far.shape[0], 512):
            put_rows(table, near_rows // parts + first, 0.5 * dot(far[first : first + 512, :], inner[...]))
        incoming[...] = jnp.zeros_like(incoming)
        table_load.wait()
        for piece in range(0, unit, PIECE):
            gather(0, rows[0], piece)

    for u in range(units + 2):
        for piece in range(0, unit, PIECE):
            if u < units:
                activate(u, piece)
                following = jnp.minimum(step * units + u + 1, steps * units - 1)
                gather(following * unit, rows[(u + 1) % 2], piece)
            if 1 <= u <= units:
                finish(u - 1, piece)
        if u < units:
            post[u * unit : (u + 1) * unit, :] = dot(hidden[u * unit : (u + 1) * unit, :], edge_outer[...])
        if u >= 2:
            scatter(u - 2)

    @pl.when(step == steps - 1)
    def _():
        for load in node_loads:
            load.wait()
        post[:nodes, :] = 0.5 * dot(incoming[...].astype(BF16), node_inner[...]) + node_part[...]
        for at in range(0, nodes, PIECE):
            hidden[at : at + PIECE, :] = half_silu(post[at : at + PIECE, :]).astype(BF16)
        post[:nodes, :] = dot(hidden[:nodes, :], node_outer[...])
        for at in range(0, nodes, PIECE):
            change = layer_norm(post[at : at + PIECE, :] + node_offset[...], node_gain[...], node_shift[...])
            node_new[at : at + PIECE, :] = (node[at : at + PIECE, :].astype(F32) + change).astype(BF16)


def update(
    sender, receiver, pre, edge_lat, node_lat, far, table, node_part, inner, edge_outer, node_inner, node_outer, vectors
):
    edges, width = edge_lat.shape
    nodes = node_lat.shape[0]
    parts = width // LANES
    unit = 512
    block = 1024
    steps = edges // block
    once = pl.Buffered(1)
    hbm = pl.BlockSpec(memory_space=pl.ANY)

    def whole(array):
        return pl.BlockSpec(array.shape, lambda i, ids: (0,) * array.ndim, pipeline_mode=once)

    rows = pl.BlockSpec((block, width), lambda i, ids: (i, 0))
    row_ids = pl.BlockSpec((1, 1, block), lambda i, ids: (i, 0, 0))
    sender_part = pl.BlockSpec((width, width), lambda i, ids: (1, 0), pipeline_mode=once)
    edge_offset, edge_gain, edge_shift, node_offset, node_gain, node_shift = vectors
    vector = whole(edge_offset)
    return pl.pallas_call(
        update_kernel,
        grid_spec=pltpu.PrefetchScalarGridSpec(
            num_scalar_prefetch=1,
            grid=(steps,),
            in_specs=[row_ids, rows, rows, whole(far), sender_part, whole(edge_outer)]
            + [vector] * 3 + [hbm] * 5 + [vector] * 3,
            out_specs=[rows, pl.BlockSpec((nodes, width), lambda i, ids: (0, 0))],
            scratch_shapes=[
                pltpu.VMEM((table.shape[0] + far.shape[0] * parts, LANES), F32),
                pltpu.VMEM((nodes, width), F32),
                pltpu.VMEM((block, width), BF16),
                pltpu.VMEM((block, width), F32),
                pltpu.VMEM((block, width), BF16),
                pltpu.VMEM((unit * parts, LANES), F32),
                pltpu.VMEM((unit * parts, LANES), F32),
                pltpu.VMEM((nodes, width), BF16),
                pltpu.VMEM((nodes, width), F32),
                pltpu.VMEM((width, width), BF16),
                pltpu.VMEM((width, width), BF16),
                pltpu.SemaphoreType.DMA((5,)),
            ],
        ),
        out_shape=[
            jax.ShapeDtypeStruct((edges, width), BF16),
            jax.ShapeDtypeStruct((nodes, width), BF16),
        ],
        compiler_params=pltpu.CompilerParams(vmem_limit_bytes=VMEM_BYTES),
        name="update",
    )(
        sender, receiver.reshape(steps, 1, block), pre, edge_lat, far, inner,
        edge_outer, edge_offset, edge_gain, edge_shift,
        table, node_lat, node_part, node_inner, node_outer, node_offset, node_gain, node_shift,
    )


def solution(mesh):
    n_row, n_col = mesh.shape["row"], mesh.shape["col"]

    def shards(
        node_lat, edge_lat, near_send, far_send, edge_sender, edge_receiver,
        edge_inner, edge_bias, edge_outer, edge_offset, edge_gain, edge_shift,
        node_inner, node_bias, node_outer, node_offset, node_gain, node_shift,
    ):
        width = node_lat.shape[1]
        vectors = [
            v.reshape(1, -1) for v in (edge_offset, edge_gain, edge_shift, node_offset, node_gain, node_shift)
        ]
        pre, far, table, node_part, sender = exchange(
            n_row, n_col, far_send.swapaxes(1, 2), near_send, edge_receiver, edge_sender.reshape(-1, LANES),
            node_lat, edge_lat, edge_inner, edge_bias.reshape(1, -1), node_inner, node_bias.reshape(1, -1),
        )
        edge_new, node_new = update(
            sender.reshape(-1), edge_receiver, pre, edge_lat, node_lat, far.reshape(-1, width), table, node_part,
            edge_inner, edge_outer, node_inner, node_outer, vectors,
        )
        return edge_new, node_new

    whole = P()
    split = P(("row", "col"))
    return jax.shard_map(
        shards, mesh=mesh, in_specs=(split,) * 6 + (whole,) * 12, out_specs=(split, split), check_vma=False
    )
```

time: 51.2 us -> 47.9 us (0.936)
  Pallas kernels: 50.4 us -> 47 us
    pallas_call x1, Pallas kernels: 21.2 us -> 17.7 us  [update(): pl.pallas_call(update_kernel, grid_spec=pltpu.PrefetchScalarGridSpec(num_...]
where the time goes in v3:
time: 47.9 us; the launch traced here: 47.7 us
  Pallas kernels  47 us (98%)
  between operations  0.64 us (1%)
    pallas_call x1, Pallas kernels, exchange(): pl.pallas_call(functools.partial(exchange_kernel, n_row, n_col, block), o...  29.3 us
    pallas_call x1, Pallas kernels, update(): pl.pallas_call(update_kernel, grid_spec=pltpu.PrefetchScalarGridSpec(num_...  17.7 us

profile of v3, /device:TPU:1, one launch (start us, length us, event | category | flops | bytes accessed | tf_op | source)
XLA Modules:
  0.0 47.7 jit_solution(11507346909759208564)
XLA Ops:
  0.6 29.3 %exchange.1 = (f32[4096,512]{1,0:T(8,128)}, bf16[128,8,512]{2,1,0:T(8,128)(2,1)}, f32[2560,128]{1,0:T(8,128)}, f32[512,512]{1,0:T(8,128)}, s32[32,128]{1,0:T(8,128)}) custom-call(s32[1,8,128]{2,1,0:T(8,128)} %bitcast.17, s32[1,2,64]{2,1,0:T(2,128)} %near_ids.1, s32[4096]{0:T(1024)} %receiver.1, s32[32,128]{1,0:T(8,128)} %bitcast.15, ...), custom_call_target="tpu_custom_call" | custom-call | tf_op jit(solution)/shard_map/exchange/pallas_call | solution.py:193
  30.0 17.7 %update.1 = (bf16[4096,512]{1,0:T(8,128)(2,1)}, bf16[512,512]{1,0:T(8,128)(2,1)}) custom-call(s32[4096]{0:T(1024)} %bitcast.16, s32[4,1,1024]{2,1,0:T(1,128)} %bitcast.14, f32[4096,512]{1,0:T(8,128)} %get-tuple-element.8.pre, bf16[4096,512]{1,0:T(8,128)(2,1)} %edge.1, bf16[1024,512]{1,0:T(8,128)(2,1)} %bitcast.13, bf16[1536,512]{1,0:T(8,128)(2,1)} %inner.1, ...), custom_call_target="tpu_custom_call" | custom-call | tf_op jit(solution)/shard_map/update/pallas_call | solution.py:337

commit v4 on v3

--- a/solution.py
+++ b/solution.py
@@ -40,9 +40,10 @@
 
 def exchange_kernel(
     n_row, n_col, block,
-    far_ids, near_ids, receiver, sender, node, edge_hbm, inner_hbm, bias, node_inner_hbm, node_bias,
+    far_hbm, near_hbm, receiver_hbm, sender_hbm, node_hbm, edge_hbm, inner_hbm, bias, node_inner_hbm, node_bias,
     pre_hbm, far_out, table_out, node_out, sender_out,
     node_parts, table, near_table, picked, rows_buf, far_buf, near_buf, near_in, edge_buf, pre_buf, inner, node_inner,
+    far_ids, near_ids, receiver, sender, node,
     far_send_sem, far_recv_sem, near_send_sem, near_recv_sem, load_sem, pre_sem, out_sem,
 ):
     peers = n_row * n_col
@@ -74,14 +75,15 @@
     def greet(i):
         pl.semaphore_signal(barrier, inc=1, device_id=place(i)[1], device_id_type=MESH)
 
+    sources = (node_hbm, far_hbm, near_hbm, inner_hbm, edge_hbm, receiver_hbm, sender_hbm)
+    targets = (node, far_ids, near_ids, inner, edge_buf, receiver, sender)
+    loads = [pltpu.make_async_copy(a, b, load_sem.at[i]) for i, (a, b) in enumerate(zip(sources, targets))]
+    node_load = pltpu.make_async_copy(node_inner_hbm.at[pl.ds(0, width)], node_inner, load_sem.at[7])
+    for load in loads + [node_load]:
+        load.start()
     for_peers(greet)
-    loads = [
-        pltpu.make_async_copy(inner_hbm, inner, load_sem.at[0]),
-        pltpu.make_async_copy(edge_hbm, edge_buf, load_sem.at[1]),
-        pltpu.make_async_copy(node_inner_hbm.at[pl.ds(0, width)], node_inner, load_sem.at[2]),
-    ]
-    for load in loads:
-        load.start()
+    for load in loads[:3]:
+        load.wait()
 
     put_rows(node_parts, 0, node[...].astype(F32))
     node_rows = node_parts.reshape(nodes, parts, LANES)
@@ -135,11 +137,11 @@
 
     for_peers(send)
 
+    for load in loads[3:]:
+        load.wait()
     sender_out[...] = sender[...] * parts
-    loads[0].wait()
     put_rows(table, 0, dot(node[...], inner[2 * width :, :]))
     table_rows = table.reshape(nodes, parts, LANES)
-    loads[1].wait()
 
     def pre_copy(first):
         return pltpu.make_async_copy(pre_buf.at[pl.ds(first, block)], pre_hbm.at[pl.ds(first, block)], pre_sem)
@@ -159,7 +161,7 @@
     for first in range(0, nodes, LANES):
         values = dot(node[first : first + LANES, :], inner[width : 2 * width, :])
         put_rows(near_table, first, 0.5 * values)
-    loads[2].wait()
+    node_load.wait()
     node_out[...] = 0.5 * (dot(node[...], node_inner[...]) + node_bias[...])
     for side, copy in enumerate(near_copies):
         copy.wait()
@@ -187,7 +189,6 @@
     halo = near_send.shape[2]
     parts = width // LANES
     block = min(512, edges)
-    smem = pl.BlockSpec(memory_space=pltpu.SMEM)
     vmem = pl.BlockSpec(memory_space=pltpu.VMEM)
     hbm = pl.BlockSpec(memory_space=pl.ANY)
     return pl.pallas_call(
@@ -199,7 +200,7 @@
             jax.ShapeDtypeStruct((nodes, width), F32),
             jax.ShapeDtypeStruct(sender.shape, jnp.int32),
         ),
-        in_specs=[smem, smem, smem, vmem, vmem, hbm, hbm, vmem, hbm, vmem],
+        in_specs=[hbm] * 7 + [vmem, hbm, vmem],
         out_specs=(hbm, hbm, hbm, vmem, vmem),
         scratch_shapes=[
             pltpu.VMEM((nodes * parts, LANES), F32),
@@ -214,11 +215,16 @@
             pltpu.VMEM((edges, width), F32),
             pltpu.VMEM(inner.shape, BF16),
             pltpu.VMEM((width, width), BF16),
+            pltpu.SMEM(far_send.shape, jnp.int32),
+            pltpu.SMEM(near_send.shape, jnp.int32),
+            pltpu.SMEM(receiver.shape, jnp.int32),
+            pltpu.VMEM(sender.shape, jnp.int32),
+            pltpu.VMEM(node_lat.shape, BF16),
             pltpu.SemaphoreType.DMA,
             pltpu.SemaphoreType.DMA,
             pltpu.SemaphoreType.DMA((2,)),
             pltpu.SemaphoreType.DMA((2,)),
-            pltpu.SemaphoreType.DMA((3,)),
+            pltpu.SemaphoreType.DMA((8,)),
             pltpu.SemaphoreType.DMA,
             pltpu.SemaphoreType.DMA,
         ],
@@ -230,69 +236,100 @@
 
 
 def update_kernel(
-    sender, receiver, pre, edge, far, inner, edge_outer, edge_offset, edge_gain, edge_shift,
-    table_hbm, node_hbm, node_part_hbm, node_inner_hbm, node_outer_hbm, node_offset, node_gain, node_shift,
+    sender, receiver, edge_offset, edge_gain, edge_shift, node_offset, node_gain, node_shift,
+    pre_hbm, edge_hbm, far_hbm, inner_hbm, edge_outer_hbm,
+    table_hbm, node_hbm, node_part_hbm, node_inner_hbm, node_outer_hbm,
     edge_new, node_new,
-    table, incoming, hidden, post, message, rows_a, rows_b, node, node_part, node_inner, node_outer, load_sem,
+    table, incoming, hidden, post, message, rows_a, rows_b, pre, edge, far, inner, edge_outer,
+    node, node_part, node_inner, node_outer, load_sem, pre_sem, edge_sem, out_sem,
 ):
     step, steps = pl.program_id(0), pl.num_programs(0)
-    block, width = edge.shape
+    edges, width = edge.shape
     nodes = node.shape[0]
     parts = width // LANES
-    unit = rows_a.shape[0] // parts
-    units = block // unit
+    all_units, _, unit = receiver.shape
+    units = hidden.shape[0] // unit
     rows = (rows_a, rows_b)
     near_rows = table_hbm.shape[0]
 
-    table_load = pltpu.make_async_copy(table_hbm, table.at[pl.ds(0, near_rows)], load_sem.at[0])
+    copy = pltpu.make_async_copy
+    table_load = copy(table_hbm, table.at[pl.ds(0, near_rows)], load_sem.at[0])
+    far_load = copy(far_hbm, far, load_sem.at[1])
+    inner_load = copy(inner_hbm.at[pl.ds(width, width)], inner, load_sem.at[2])
+    outer_load = copy(edge_outer_hbm, edge_outer, load_sem.at[3])
     node_loads = [
-        pltpu.make_async_copy(node_inner_hbm.at[pl.ds(width, width)], node_inner, load_sem.at[1]),
-        pltpu.make_async_copy(node_outer_hbm, node_outer, load_sem.at[2]),
-        pltpu.make_async_copy(node_hbm, node, load_sem.at[3]),
-        pltpu.make_async_copy(node_part_hbm, node_part, load_sem.at[4]),
+        copy(node_inner_hbm.at[pl.ds(width, width)], node_inner, load_sem.at[4]),
+        copy(node_outer_hbm, node_outer, load_sem.at[5]),
+        copy(node_hbm, node, load_sem.at[6]),
+        copy(node_part_hbm, node_part, load_sem.at[7]),
     ]
+
+    def part_of(ref, u):
+        return ref.at[pl.ds(pl.multiple_of(u * unit, unit), unit)]
+
+    def pre_load(u):
+        return copy(part_of(pre_hbm, u), part_of(pre, u), pre_sem.at[u])
+
+    def edge_load(u):
+        return copy(part_of(edge_hbm, u), part_of(edge, u), edge_sem.at[u])
+
+    def edge_store(u):
+        return copy(part_of(edge, u), part_of(edge_new, u), out_sem.at[u])
 
     def gather(first, buffer, piece):
         for j in range(piece, piece + PIECE):
             start = pl.multiple_of(sender[first + j], parts)
             buffer[pl.ds(j * parts, parts), :] = table[pl.ds(start, parts), :]
+
+    base = pl.multiple_of(step * (units * unit), units * unit)
 
     def activate(u, piece):
         at = u * unit + piece
         for k in range(parts):
             lanes = slice(k * LANES, (k + 1) * LANES)
             near = rows[u % 2][pl.ds(piece * parts + k, PIECE, stride=parts), :]
-            hidden[at : at + PIECE, lanes] = half_silu(pre[at : at + PIECE, lanes] + near).astype(BF16)
+            half = pre[pl.ds(base + at, PIECE), lanes] + near
+            hidden[at : at + PIECE, lanes] = half_silu(half).astype(BF16)
 
     def finish(u, piece):
         at = u * unit + piece
         values = layer_norm(post[at : at + PIECE, :] + edge_offset[...], edge_gain[...], edge_shift[...]).astype(BF16)
         message[at : at + PIECE, :] = values
-        edge_new[at : at + PIECE, :] = edge[at : at + PIECE, :] + values
+        edge[pl.ds(base + at, PIECE), :] = edge[pl.ds(base + at, PIECE), :] + values
 
     def scatter(u):
-        ids = receiver[0, :, u * unit : (u + 1) * unit].astype(jnp.int16)
+        ids = receiver[step * units + u].astype(jnp.int16)
         node_ids = lax.broadcasted_iota(jnp.int16, (nodes, unit), 0)
         hot = jnp.where(node_ids == ids, jnp.bfloat16(1), jnp.bfloat16(0))
         incoming[...] += dot(hot, message[u * unit : (u + 1) * unit, :])
 
     @pl.when(step == 0)
     def _():
-        table_load.start()
+        for load in (inner_load, far_load, table_load, pre_load(0), outer_load, edge_load(0)):
+            load.start()
+        for u in range(1, all_units):
+            pre_load(u).start()
+            edge_load(u).start()
         for load in node_loads:
             load.start()
+        incoming[...] = jnp.zeros_like(incoming)
+        inner_load.wait()
+        far_load.wait()
         for first in range(0, far.shape[0], 512):
             put_rows(table, near_rows // parts + first, 0.5 * dot(far[first : first + 512, :], inner[...]))
-        incoming[...] = jnp.zeros_like(incoming)
         table_load.wait()
         for piece in range(0, unit, PIECE):
             gather(0, rows[0], piece)
-
+        outer_load.wait()
+
+    for u in range(units):
+        pre_load(step * units + u).wait()
+        edge_load(step * units + u).wait()
     for u in range(units + 2):
         for piece in range(0, unit, PIECE):
             if u < units:
                 activate(u, piece)
-                following = jnp.minimum(step * units + u + 1, steps * units - 1)
+                following = jnp.minimum(step * units + u + 1, all_units - 1)
                 gather(following * unit, rows[(u + 1) % 2], piece)
             if 1 <= u <= units:
                 finish(u - 1, piece)
@@ -300,6 +337,8 @@
             post[u * unit : (u + 1) * unit, :] = dot(hidden[u * unit : (u + 1) * unit, :], edge_outer[...])
         if u >= 2:
             scatter(u - 2)
+    for u in range(units):
+        edge_store(step * units + u).start()
 
     @pl.when(step == steps - 1)
     def _():
@@ -312,6 +351,8 @@
         for at in range(0, nodes, PIECE):
             change = layer_norm(post[at : at + PIECE, :] + node_offset[...], node_gain[...], node_shift[...])
             node_new[at : at + PIECE, :] = (node[at : at + PIECE, :].astype(F32) + change).astype(BF16)
+        for u in range(all_units):
+            edge_store(u).wait()
 
 
 def update(
@@ -323,25 +364,17 @@
     unit = 512
     block = 1024
     steps = edges // block
-    once = pl.Buffered(1)
+    all_units = edges // unit
     hbm = pl.BlockSpec(memory_space=pl.ANY)
-
-    def whole(array):
-        return pl.BlockSpec(array.shape, lambda i, ids: (0,) * array.ndim, pipeline_mode=once)
-
-    rows = pl.BlockSpec((block, width), lambda i, ids: (i, 0))
-    row_ids = pl.BlockSpec((1, 1, block), lambda i, ids: (i, 0, 0))
-    sender_part = pl.BlockSpec((width, width), lambda i, ids: (1, 0), pipeline_mode=once)
-    edge_offset, edge_gain, edge_shift, node_offset, node_gain, node_shift = vectors
-    vector = whole(edge_offset)
+    vector = pl.BlockSpec((1, width), lambda i, ids: (0, 0), pipeline_mode=pl.Buffered(1))
     return pl.pallas_call(
         update_kernel,
         grid_spec=pltpu.PrefetchScalarGridSpec(
             num_scalar_prefetch=1,
             grid=(steps,),
-            in_specs=[row_ids, rows, rows, whole(far), sender_part, whole(edge_outer)]
-            + [vector] * 3 + [hbm] * 5 + [vector] * 3,
-            out_specs=[rows, pl.BlockSpec((nodes, width), lambda i, ids: (0, 0))],
+            in_specs=[pl.BlockSpec((all_units, 1, unit), lambda i, ids: (0, 0, 0), pipeline_mode=pl.Buffered(1))]
+            + [vector] * 6 + [hbm] * 10,
+            out_specs=[hbm, pl.BlockSpec((nodes, width), lambda i, ids: (0, 0))],
             scratch_shapes=[
                 pltpu.VMEM((table.shape[0] + far.shape[0] * parts, LANES), F32),
                 pltpu.VMEM((nodes, width), F32),
@@ -350,11 +383,19 @@
                 pltpu.VMEM((block, width), BF16),
                 pltpu.VMEM((unit * parts, LANES), F32),
                 pltpu.VMEM((unit * parts, LANES), F32),
+                pltpu.VMEM((edges, width), F32),
+                pltpu.VMEM((edges, width), BF16),
+                pltpu.VMEM(far.shape, BF16),
+                pltpu.VMEM((width, width), BF16),
+                pltpu.VMEM((width, width), BF16),
                 pltpu.VMEM((nodes, width), BF16),
                 pltpu.VMEM((nodes, width), F32),
                 pltpu.VMEM((width, width), BF16),
                 pltpu.VMEM((width, width), BF16),
-                pltpu.SemaphoreType.DMA((5,)),
+                pltpu.SemaphoreType.DMA((8,)),
+                pltpu.SemaphoreType.DMA((all_units,)),
+                pltpu.SemaphoreType.DMA((all_units,)),
+                pltpu.SemaphoreType.DMA((all_units,)),
             ],
         ),
         out_shape=[
@@ -364,9 +405,8 @@
         compiler_params=pltpu.CompilerParams(vmem_limit_bytes=VMEM_BYTES),
         name="update",
     )(
-        sender, receiver.reshape(steps, 1, block), pre, edge_lat, far, inner,
-        edge_outer, edge_offset, edge_gain, edge_shift,
-        table, node_lat, node_part, node_inner, node_outer, node_offset, node_gain, node_shift,
+        sender, receiver.reshape(all_units, 1, unit), *vectors,
+        pre, edge_lat, far, inner, edge_outer, table, node_lat, node_part, node_inner, node_outer,
     )
 
 

time: 47.9 us -> 47 us (0.981)
  Pallas kernels: 47 us -> 46.1 us
    pallas_call x1, Pallas kernels: 29.3 us -> 28.8 us  [exchange(): pl.pallas_call(functools.partial(exchange_kernel, n_row, n_col, block), o...]
where the time goes in v4:
time: 47 us; the launch traced here: 46.8 us
  Pallas kernels  46.1 us (98%)
  between operations  0.64 us (1%)
    pallas_call x1, Pallas kernels, exchange(): pl.pallas_call(functools.partial(exchange_kernel, n_row, n_col, block), o...  28.8 us
    pallas_call x1, Pallas kernels, update(): pl.pallas_call(update_kernel, grid_spec=pltpu.PrefetchScalarGridSpec(num_...  17.3 us

profile of v4, /device:TPU:1, one launch (start us, length us, event | category | flops | bytes accessed | tf_op | source)
XLA Modules:
  0.0 46.8 jit_solution(10790555598946425014)
XLA Ops:
  0.6 28.8 %exchange.1 = (f32[4096,512]{1,0:T(8,128)}, bf16[128,8,512]{2,1,0:T(8,128)(2,1)}, f32[2560,128]{1,0:T(8,128)}, f32[512,512]{1,0:T(8,128)}, s32[32,128]{1,0:T(8,128)}) custom-call(s32[1,8,128]{2,1,0:T(8,128)} %bitcast.17, s32[1,2,64]{2,1,0:T(2,128)} %near_hbm.1, s32[4096]{0:T(1024)} %receiver_hbm.1, s32[32,128]{1,0:T(8,128)} %bitcast.15, ...), custom_call_target="tpu_custom_call" | custom-call | tf_op jit(solution)/shard_map/exchange/pallas_call | solution.py:194
  29.5 17.3 %update.1 = (bf16[4096,512]{1,0:T(8,128)(2,1)}, bf16[512,512]{1,0:T(8,128)(2,1)}) custom-call(s32[4096]{0:T(1024)} %bitcast.16, s32[8,1,512]{2,1,0:T(1,128)} %bitcast.14, f32[1,512]{1,0:T(1,128)} %bitcast.20, f32[1,512]{1,0:T(1,128)} %bitcast.21, f32[1,512]{1,0:T(1,128)} %bitcast.22, f32[1,512]{1,0:T(1,128)} %bitcast.23, f32[1,512]{1,0:T(1,128)} %bitcast.24, ...), custom_call_target="tpu_custom_call" | custom-call | tf_op jit(solution)/shard_map/update/pallas_call | solution.py:370

commit v5 on v4

--- a/solution.py
+++ b/solution.py
@@ -13,7 +13,8 @@
 LANES = 128
 PIECE = 64
 UNROLL = 8
-VMEM_BYTES = 60 * 1024 * 1024
+EXCHANGE_BYTES = 45000 << 10
+UPDATE_BYTES = 45000 << 10
 
 
 def dot(a, b):
@@ -40,11 +41,11 @@
 
 def exchange_kernel(
     n_row, n_col, block,
-    far_hbm, near_hbm, receiver_hbm, sender_hbm, node_hbm, edge_hbm, inner_hbm, bias, node_inner_hbm, node_bias,
-    pre_hbm, far_out, table_out, node_out, sender_out,
-    node_parts, table, near_table, picked, rows_buf, far_buf, near_buf, near_in, edge_buf, pre_buf, inner, node_inner,
-    far_ids, near_ids, receiver, sender, node,
-    far_send_sem, far_recv_sem, near_send_sem, near_recv_sem, load_sem, pre_sem, out_sem,
+    far_hbm, near_hbm, receiver_hbm, sender_hbm, node_hbm, edge_hbm, inner_hbm, bias_hbm, node_inner_hbm, node_bias_hbm,
+    pre, edge_buf, far_out, near_table, node_out, sender_out,
+    node_parts, table, picked, rows_buf, far_buf, near_buf, near_in, inner, node_inner,
+    far_ids, near_ids, receiver, sender, node, bias, node_bias,
+    far_send_sem, far_recv_sem, near_send_sem, near_recv_sem, load_sem,
 ):
     peers = n_row * n_col
     row, col = lax.axis_index("row"), lax.axis_index("col")
@@ -75,10 +76,10 @@
     def greet(i):
         pl.semaphore_signal(barrier, inc=1, device_id=place(i)[1], device_id_type=MESH)
 
-    sources = (node_hbm, far_hbm, near_hbm, inner_hbm, edge_hbm, receiver_hbm, sender_hbm)
-    targets = (node, far_ids, near_ids, inner, edge_buf, receiver, sender)
+    sources = (node_hbm, far_hbm, near_hbm, inner_hbm, edge_hbm, receiver_hbm, sender_hbm, bias_hbm, node_bias_hbm)
+    targets = (node, far_ids, near_ids, inner, edge_buf, receiver, sender, bias, node_bias)
     loads = [pltpu.make_async_copy(a, b, load_sem.at[i]) for i, (a, b) in enumerate(zip(sources, targets))]
-    node_load = pltpu.make_async_copy(node_inner_hbm.at[pl.ds(0, width)], node_inner, load_sem.at[7])
+    node_load = pltpu.make_async_copy(node_inner_hbm.at[pl.ds(0, width)], node_inner, load_sem.at[9])
     for load in loads + [node_load]:
         load.start()
     for_peers(greet)
@@ -143,17 +144,13 @@
     put_rows(table, 0, dot(node[...], inner[2 * width :, :]))
     table_rows = table.reshape(nodes, parts, LANES)
 
-    def pre_copy(first):
-        return pltpu.make_async_copy(pre_buf.at[pl.ds(first, block)], pre_hbm.at[pl.ds(first, block)], pre_sem)
-
     def first_layer(i, carry):
         first = pl.multiple_of(i * block, block)
         for j in range(block):
             rows_buf[pl.ds(j * parts, parts), :] = table_rows[receiver[first + j]]
         rows = jnp.concatenate([rows_buf[pl.ds(k, block, stride=parts), :] for k in range(parts)], axis=1)
         total = dot(edge_buf[pl.ds(first, block), :], inner[:width, :]) + rows + bias[...]
-        pre_buf[pl.ds(first, block), :] = 0.5 * total
-        pre_copy(first).start()
+        pre[pl.ds(first, block), :] = 0.5 * total
         return carry
 
     lax.fori_loop(0, edges // block, first_layer, 0)
@@ -167,11 +164,6 @@
         copy.wait()
         values = dot(near_in[side], inner[width : 2 * width, :])
         put_rows(near_table, nodes + side * halo, 0.5 * values)
-    table_copy = pltpu.make_async_copy(near_table, table_out, out_sem)
-    table_copy.start()
-
-    pltpu.make_async_copy(pre_buf, pre_hbm, pre_sem).wait()
-    table_copy.wait()
     pltpu.make_async_copy(
         far_out.at[pl.ds(0, peers - 1)], far_out.at[pl.ds(0, peers - 1)], far_recv_sem
     ).wait()
@@ -190,29 +182,28 @@
     parts = width // LANES
     block = min(512, edges)
     vmem = pl.BlockSpec(memory_space=pltpu.VMEM)
-    hbm = pl.BlockSpec(memory_space=pl.ANY)
+    hbm = pl.BlockSpec(memory_space=pltpu.HBM)
+    anywhere = pl.BlockSpec(memory_space=pl.ANY)
     return pl.pallas_call(
         functools.partial(exchange_kernel, n_row, n_col, block),
         out_shape=(
-            jax.ShapeDtypeStruct((edges, width), F32),
+            pltpu.VMEM((edges, width), F32),
+            pltpu.VMEM((edges, width), BF16),
             jax.ShapeDtypeStruct((peers, slots, width), BF16),
-            jax.ShapeDtypeStruct(((nodes + 2 * halo) * parts, LANES), F32),
-            jax.ShapeDtypeStruct((nodes, width), F32),
+            pltpu.VMEM(((nodes + 2 * halo) * parts, LANES), F32),
+            pltpu.VMEM((nodes, width), F32),
             jax.ShapeDtypeStruct(sender.shape, jnp.int32),
         ),
-        in_specs=[hbm] * 7 + [vmem, hbm, vmem],
-        out_specs=(hbm, hbm, hbm, vmem, vmem),
+        in_specs=[hbm] * 10,
+        out_specs=(vmem, vmem, anywhere, vmem, vmem, vmem),
         scratch_shapes=[
             pltpu.VMEM((nodes * parts, LANES), F32),
             pltpu.VMEM((nodes * parts, LANES), F32),
-            pltpu.VMEM(((nodes + 2 * halo) * parts, LANES), F32),
             pltpu.VMEM((4, 16 * parts, LANES), F32),
             pltpu.VMEM((block * parts, LANES), F32),
             pltpu.VMEM((peers, slots, width), BF16),
             pltpu.VMEM((2, halo, width), BF16),
             pltpu.VMEM((2, halo, width), BF16),
-            pltpu.VMEM((edges, width), BF16),
-            pltpu.VMEM((edges, width), F32),
             pltpu.VMEM(inner.shape, BF16),
             pltpu.VMEM((width, width), BF16),
             pltpu.SMEM(far_send.shape, jnp.int32),
@@ -220,16 +211,16 @@
             pltpu.SMEM(receiver.shape, jnp.int32),
             pltpu.VMEM(sender.shape, jnp.int32),
             pltpu.VMEM(node_lat.shape, BF16),
+            pltpu.VMEM(bias.shape, F32),
+            pltpu.VMEM(node_bias.shape, F32),
             pltpu.SemaphoreType.DMA,
             pltpu.SemaphoreType.DMA,
             pltpu.SemaphoreType.DMA((2,)),
             pltpu.SemaphoreType.DMA((2,)),
-            pltpu.SemaphoreType.DMA((8,)),
-            pltpu.SemaphoreType.DMA,
-            pltpu.SemaphoreType.DMA,
+            pltpu.SemaphoreType.DMA((10,)),
         ],
         compiler_params=pltpu.CompilerParams(
-            collective_id=0, has_side_effects=True, vmem_limit_bytes=VMEM_BYTES
+            collective_id=0, has_side_effects=True, vmem_limit_bytes=EXCHANGE_BYTES
         ),
         name="exchange",
     )(far_send, near_send, receiver, sender, node_lat, edge_lat, inner, bias, node_inner, node_bias)
@@ -237,11 +228,10 @@
 
 def update_kernel(
     sender, receiver, edge_offset, edge_gain, edge_shift, node_offset, node_gain, node_shift,
-    pre_hbm, edge_hbm, far_hbm, inner_hbm, edge_outer_hbm,
-    table_hbm, node_hbm, node_part_hbm, node_inner_hbm, node_outer_hbm,
+    pre, edge, far, near_table, node_part, inner_hbm, edge_outer_hbm, node_hbm, node_inner_hbm, node_outer_hbm,
     edge_new, node_new,
-    table, incoming, hidden, post, message, rows_a, rows_b, pre, edge, far, inner, edge_outer,
-    node, node_part, node_inner, node_outer, load_sem, pre_sem, edge_sem, out_sem,
+    table, incoming, hidden, post, message, rows_a, rows_b, edge_out, inner, edge_outer,
+    node, node_inner, node_outer, load_sem, out_sem,
 ):
     step, steps = pl.program_id(0), pl.num_programs(0)
     edges, width = edge.shape
@@ -250,31 +240,23 @@
     all_units, _, unit = receiver.shape
     units = hidden.shape[0] // unit
     rows = (rows_a, rows_b)
-    near_rows = table_hbm.shape[0]
+    near_rows = near_table.shape[0]
 
     copy = pltpu.make_async_copy
-    table_load = copy(table_hbm, table.at[pl.ds(0, near_rows)], load_sem.at[0])
-    far_load = copy(far_hbm, far, load_sem.at[1])
+    table_load = copy(near_table, table.at[pl.ds(0, near_rows)], load_sem.at[0])
     inner_load = copy(inner_hbm.at[pl.ds(width, width)], inner, load_sem.at[2])
     outer_load = copy(edge_outer_hbm, edge_outer, load_sem.at[3])
     node_loads = [
         copy(node_inner_hbm.at[pl.ds(width, width)], node_inner, load_sem.at[4]),
         copy(node_outer_hbm, node_outer, load_sem.at[5]),
         copy(node_hbm, node, load_sem.at[6]),
-        copy(node_part_hbm, node_part, load_sem.at[7]),
     ]
 
     def part_of(ref, u):
         return ref.at[pl.ds(pl.multiple_of(u * unit, unit), unit)]
 
-    def pre_load(u):
-        return copy(part_of(pre_hbm, u), part_of(pre, u), pre_sem.at[u])
-
-    def edge_load(u):
-        return copy(part_of(edge_hbm, u), part_of(edge, u), edge_sem.at[u])
-
     def edge_store(u):
-        return copy(part_of(edge, u), part_of(edge_new, u), out_sem.at[u])
+        return copy(part_of(edge_out, u), part_of(edge_new, u), out_sem.at[u])
 
     def gather(first, buffer, piece):
         for j in range(piece, piece + PIECE):
@@ -295,7 +277,7 @@
         at = u * unit + piece
         values = layer_norm(post[at : at + PIECE, :] + edge_offset[...], edge_gain[...], edge_shift[...]).astype(BF16)
         message[at : at + PIECE, :] = values
-        edge[pl.ds(base + at, PIECE), :] = edge[pl.ds(base + at, PIECE), :] + values
+        edge_out[pl.ds(base + at, PIECE), :] = edge[pl.ds(base + at, PIECE), :] + values
 
     def scatter(u):
         ids = receiver[step * units + u].astype(jnp.int16)
@@ -305,16 +287,10 @@
 
     @pl.when(step == 0)
     def _():
-        for load in (inner_load, far_load, table_load, pre_load(0), outer_load, edge_load(0)):
-            load.start()
-        for u in range(1, all_units):
-            pre_load(u).start()
-            edge_load(u).start()
-        for load in node_loads:
+        for load in [inner_load, table_load, outer_load] + node_loads:
             load.start()
         incoming[...] = jnp.zeros_like(incoming)
         inner_load.wait()
-        far_load.wait()
         for first in range(0, far.shape[0], 512):
             put_rows(table, near_rows // parts + first, 0.5 * dot(far[first : first + 512, :], inner[...]))
         table_load.wait()
@@ -322,9 +298,6 @@
             gather(0, rows[0], piece)
         outer_load.wait()
 
-    for u in range(units):
-        pre_load(step * units + u).wait()
-        edge_load(step * units + u).wait()
     for u in range(units + 2):
         for piece in range(0, unit, PIECE):
             if u < units:
@@ -365,7 +338,8 @@
     block = 1024
     steps = edges // block
     all_units = edges // unit
-    hbm = pl.BlockSpec(memory_space=pl.ANY)
+    hbm = pl.BlockSpec(memory_space=pltpu.HBM)
+    vmem = pl.BlockSpec(memory_space=pltpu.VMEM)
     vector = pl.BlockSpec((1, width), lambda i, ids: (0, 0), pipeline_mode=pl.Buffered(1))
     return pl.pallas_call(
         update_kernel,
@@ -373,8 +347,8 @@
             num_scalar_prefetch=1,
             grid=(steps,),
             in_specs=[pl.BlockSpec((all_units, 1, unit), lambda i, ids: (0, 0, 0), pipeline_mode=pl.Buffered(1))]
-            + [vector] * 6 + [hbm] * 10,
-            out_specs=[hbm, pl.BlockSpec((nodes, width), lambda i, ids: (0, 0))],
+            + [vector] * 6 + [vmem] * 5 + [hbm] * 5,
+            out_specs=[pl.BlockSpec(memory_space=pl.ANY), pl.BlockSpec((nodes, width), lambda i, ids: (0, 0))],
             scratch_shapes=[
                 pltpu.VMEM((table.shape[0] + far.shape[0] * parts, LANES), F32),
                 pltpu.VMEM((nodes, width), F32),
@@ -383,18 +357,13 @@
                 pltpu.VMEM((block, width), BF16),
                 pltpu.VMEM((unit * parts, LANES), F32),
                 pltpu.VMEM((unit * parts, LANES), F32),
-                pltpu.VMEM((edges, width), F32),
                 pltpu.VMEM((edges, width), BF16),
-                pltpu.VMEM(far.shape, BF16),
                 pltpu.VMEM((width, width), BF16),
                 pltpu.VMEM((width, width), BF16),
                 pltpu.VMEM((nodes, width), BF16),
-                pltpu.VMEM((nodes, width), F32),
                 pltpu.VMEM((width, width), BF16),
                 pltpu.VMEM((width, width), BF16),
                 pltpu.SemaphoreType.DMA((8,)),
-                pltpu.SemaphoreType.DMA((all_units,)),
-                pltpu.SemaphoreType.DMA((all_units,)),
                 pltpu.SemaphoreType.DMA((all_units,)),
             ],
         ),
@@ -402,11 +371,11 @@
             jax.ShapeDtypeStruct((edges, width), BF16),
             jax.ShapeDtypeStruct((nodes, width), BF16),
         ],
-        compiler_params=pltpu.CompilerParams(vmem_limit_bytes=VMEM_BYTES),
+        compiler_params=pltpu.CompilerParams(vmem_limit_bytes=UPDATE_BYTES),
         name="update",
     )(
         sender, receiver.reshape(all_units, 1, unit), *vectors,
-        pre, edge_lat, far, inner, edge_outer, table, node_lat, node_part, node_inner, node_outer,
+        pre, edge_lat, far, table, node_part, inner, edge_outer, node_lat, node_inner, node_outer,
     )
 
 
@@ -422,12 +391,15 @@
         vectors = [
             v.reshape(1, -1) for v in (edge_offset, edge_gain, edge_shift, node_offset, node_gain, node_shift)
         ]
-        pre, far, table, node_part, sender = exchange(
+        pre, edge_copy, far, table, node_part, sender = exchange(
             n_row, n_col, far_send.swapaxes(1, 2), near_send, edge_receiver, edge_sender.reshape(-1, LANES),
             node_lat, edge_lat, edge_inner, edge_bias.reshape(1, -1), node_inner, node_bias.reshape(1, -1),
         )
+        pre, edge_copy, table, node_part = [
+            pltpu.with_memory_space_constraint(array, pltpu.VMEM) for array in (pre, edge_copy, table, node_part)
+        ]
         edge_new, node_new = update(
-            sender.reshape(-1), edge_receiver, pre, edge_lat, node_lat, far.reshape(-1, width), table, node_part,
+            sender.reshape(-1), edge_receiver, pre, edge_copy, node_lat, far.reshape(-1, width), table, node_part,
             edge_inner, edge_outer, node_inner, node_outer, vectors,
         )
         return edge_new, node_new

time: 47 us -> 44.8 us (0.953)
  Pallas kernels: 46.1 us -> 43.9 us
    pallas_call x1, Pallas kernels: 17.3 us -> 16.1 us  [update(): pl.pallas_call(update_kernel, grid_spec=pltpu.PrefetchScalarGridSpec(num_...]
    pallas_call x1, Pallas kernels: 28.8 us -> 27.8 us  [exchange(): pl.pallas_call(functools.partial(exchange_kernel, n_row, n_col, block), o...]
where the time goes in v5:
time: 44.8 us; the launch traced here: 44.6 us
  Pallas kernels  43.9 us (98%)
  between operations  0.64 us (1%)
    pallas_call x1, Pallas kernels, exchange(): pl.pallas_call(functools.partial(exchange_kernel, n_row, n_col, block), o...  27.8 us
    pallas_call x1, Pallas kernels, update(): pl.pallas_call(update_kernel, grid_spec=pltpu.PrefetchScalarGridSpec(num_...  16.1 us

profile of v5, /device:TPU:1, one launch (start us, length us, event | category | flops | bytes accessed | tf_op | source)
XLA Modules:
  0.0 44.6 jit_solution(17813437565525105131)
XLA Ops:
  0.6 27.8 %exchange.1 = (f32[4096,512]{1,0:T(8,128)S(1)}, bf16[4096,512]{1,0:T(8,128)(2,1)S(1)}, bf16[128,8,512]{2,1,0:T(8,128)(2,1)}, f32[2560,128]{1,0:T(8,128)S(1)}, f32[512,512]{1,0:T(8,128)S(1)}, /*index=5*/s32[32,128]{1,0:T(8,128)}) custom-call(s32[1,8,128]{2,1,0:T(8,128)} %bitcast.17, s32[1,2,64]{2,1,0:T(2,128)} %near_hbm.1, s32[4096]{0:T(1024)} %receiver_hbm.1, ...), custom_call_target="tpu_custom_call" | custom-call | tf_op jit(solution)/shard_map/exchange/pallas_call | solution.py:187
  28.5 16.1 %update.1 = (bf16[4096,512]{1,0:T(8,128)(2,1)}, bf16[512,512]{1,0:T(8,128)(2,1)}) custom-call(s32[4096]{0:T(1024)} %bitcast.16, s32[8,1,512]{2,1,0:T(1,128)} %bitcast.14, f32[1,512]{1,0:T(1,128)} %bitcast.20, f32[1,512]{1,0:T(1,128)} %bitcast.21, f32[1,512]{1,0:T(1,128)} %bitcast.22, f32[1,512]{1,0:T(1,128)} %bitcast.23, f32[1,512]{1,0:T(1,128)} %bitcast.24, ...), custom_call_target="tpu_custom_call" | custom-call | tf_op jit(solution)/shard_map/update/pallas_call | solution.py:344

commit v6 on v5

--- a/solution.py
+++ b/solution.py
@@ -13,8 +13,8 @@
 LANES = 128
 PIECE = 64
 UNROLL = 8
-EXCHANGE_BYTES = 45000 << 10
-UPDATE_BYTES = 45000 << 10
+EXCHANGE_BYTES = 42000 << 10
+UPDATE_BYTES = 42000 << 10
 
 
 def dot(a, b):
@@ -42,9 +42,10 @@
 def exchange_kernel(
     n_row, n_col, block,
     far_hbm, near_hbm, receiver_hbm, sender_hbm, node_hbm, edge_hbm, inner_hbm, bias_hbm, node_inner_hbm, node_bias_hbm,
-    pre, edge_buf, far_out, near_table, node_out, sender_out,
-    node_parts, table, picked, rows_buf, far_buf, near_buf, near_in, inner, node_inner,
-    far_ids, near_ids, receiver, sender, node, bias, node_bias,
+    edge_outer_hbm, node_outer_hbm,
+    pre, edge_buf, far_out, near_table, node_out, inner, edge_outer, node, node_low, node_outer, sender_out,
+    node_parts, table, picked, rows_buf, far_buf, near_buf, near_in, node_inner,
+    far_ids, near_ids, receiver, sender, bias, node_bias,
     far_send_sem, far_recv_sem, near_send_sem, near_recv_sem, load_sem,
 ):
     peers = n_row * n_col
@@ -80,7 +81,12 @@
     targets = (node, far_ids, near_ids, inner, edge_buf, receiver, sender, bias, node_bias)
     loads = [pltpu.make_async_copy(a, b, load_sem.at[i]) for i, (a, b) in enumerate(zip(sources, targets))]
     node_load = pltpu.make_async_copy(node_inner_hbm.at[pl.ds(0, width)], node_inner, load_sem.at[9])
-    for load in loads + [node_load]:
+    later_loads = [
+        pltpu.make_async_copy(edge_outer_hbm, edge_outer, load_sem.at[10]),
+        pltpu.make_async_copy(node_outer_hbm, node_outer, load_sem.at[11]),
+        pltpu.make_async_copy(node_inner_hbm.at[pl.ds(width, width)], node_low, load_sem.at[12]),
+    ]
+    for load in loads + [node_load] + later_loads:
         load.start()
     for_peers(greet)
     for load in loads[:3]:
@@ -158,7 +164,8 @@
     for first in range(0, nodes, LANES):
         values = dot(node[first : first + LANES, :], inner[width : 2 * width, :])
         put_rows(near_table, first, 0.5 * values)
-    node_load.wait()
+    for load in [node_load] + later_loads:
+        load.wait()
     node_out[...] = 0.5 * (dot(node[...], node_inner[...]) + node_bias[...])
     for side, copy in enumerate(near_copies):
         copy.wait()
@@ -173,7 +180,8 @@
 
 
 def exchange(
-    n_row, n_col, far_send, near_send, receiver, sender, node_lat, edge_lat, inner, bias, node_inner, node_bias
+    n_row, n_col, far_send, near_send, receiver, sender, node_lat, edge_lat, inner, bias, node_inner, node_bias,
+    edge_outer, node_outer,
 ):
     nodes, width = node_lat.shape
     edges = edge_lat.shape[0]
@@ -183,19 +191,23 @@
     block = min(512, edges)
     vmem = pl.BlockSpec(memory_space=pltpu.VMEM)
     hbm = pl.BlockSpec(memory_space=pltpu.HBM)
-    anywhere = pl.BlockSpec(memory_space=pl.ANY)
     return pl.pallas_call(
         functools.partial(exchange_kernel, n_row, n_col, block),
         out_shape=(
             pltpu.VMEM((edges, width), F32),
             pltpu.VMEM((edges, width), BF16),
-            jax.ShapeDtypeStruct((peers, slots, width), BF16),
+            pltpu.VMEM((peers, slots, width), BF16),
             pltpu.VMEM(((nodes + 2 * halo) * parts, LANES), F32),
             pltpu.VMEM((nodes, width), F32),
+            pltpu.VMEM(inner.shape, BF16),
+            pltpu.VMEM(edge_outer.shape, BF16),
+            pltpu.VMEM(node_lat.shape, BF16),
+            pltpu.VMEM((width, width), BF16),
+            pltpu.VMEM(node_outer.shape, BF16),
             jax.ShapeDtypeStruct(sender.shape, jnp.int32),
         ),
-        in_specs=[hbm] * 10,
-        out_specs=(vmem, vmem, anywhere, vmem, vmem, vmem),
+        in_specs=[hbm] * 12,
+        out_specs=(vmem,) * 11,
         scratch_shapes=[
             pltpu.VMEM((nodes * parts, LANES), F32),
             pltpu.VMEM((nodes * parts, LANES), F32),
@@ -204,34 +216,31 @@
             pltpu.VMEM((peers, slots, width), BF16),
             pltpu.VMEM((2, halo, width), BF16),
             pltpu.VMEM((2, halo, width), BF16),
-            pltpu.VMEM(inner.shape, BF16),
             pltpu.VMEM((width, width), BF16),
             pltpu.SMEM(far_send.shape, jnp.int32),
             pltpu.SMEM(near_send.shape, jnp.int32),
             pltpu.SMEM(receiver.shape, jnp.int32),
             pltpu.VMEM(sender.shape, jnp.int32),
-            pltpu.VMEM(node_lat.shape, BF16),
             pltpu.VMEM(bias.shape, F32),
             pltpu.VMEM(node_bias.shape, F32),
             pltpu.SemaphoreType.DMA,
             pltpu.SemaphoreType.DMA,
             pltpu.SemaphoreType.DMA((2,)),
             pltpu.SemaphoreType.DMA((2,)),
-            pltpu.SemaphoreType.DMA((10,)),
+            pltpu.SemaphoreType.DMA((13,)),
         ],
         compiler_params=pltpu.CompilerParams(
             collective_id=0, has_side_effects=True, vmem_limit_bytes=EXCHANGE_BYTES
         ),
         name="exchange",
-    )(far_send, near_send, receiver, sender, node_lat, edge_lat, inner, bias, node_inner, node_bias)
+    )(far_send, near_send, receiver, sender, node_lat, edge_lat, inner, bias, node_inner, node_bias, edge_outer, node_outer)
 
 
 def update_kernel(
     sender, receiver, edge_offset, edge_gain, edge_shift, node_offset, node_gain, node_shift,
-    pre, edge, far, near_table, node_part, inner_hbm, edge_outer_hbm, node_hbm, node_inner_hbm, node_outer_hbm,
+    pre, edge, far, near_table, node_part, inner, edge_outer, node, node_inner, node_outer,
     edge_new, node_new,
-    table, incoming, hidden, post, message, rows_a, rows_b, edge_out, inner, edge_outer,
-    node, node_inner, node_outer, load_sem, out_sem,
+    table, incoming, hidden, post, message, rows_a, rows_b, edge_out, load_sem, out_sem,
 ):
     step, steps = pl.program_id(0), pl.num_programs(0)
     edges, width = edge.shape
@@ -244,13 +253,6 @@
 
     copy = pltpu.make_async_copy
     table_load = copy(near_table, table.at[pl.ds(0, near_rows)], load_sem.at[0])
-    inner_load = copy(inner_hbm.at[pl.ds(width, width)], inner, load_sem.at[2])
-    outer_load = copy(edge_outer_hbm, edge_outer, load_sem.at[3])
-    node_loads = [
-        copy(node_inner_hbm.at[pl.ds(width, width)], node_inner, load_sem.at[4]),
-        copy(node_outer_hbm, node_outer, load_sem.at[5]),
-        copy(node_hbm, node, load_sem.at[6]),
-    ]
 
     def part_of(ref, u):
         return ref.at[pl.ds(pl.multiple_of(u * unit, unit), unit)]
@@ -287,16 +289,15 @@
 
     @pl.when(step == 0)
     def _():
-        for load in [inner_load, table_load, outer_load] + node_loads:
-            load.start()
+        table_load.start()
         incoming[...] = jnp.zeros_like(incoming)
-        inner_load.wait()
-        for first in range(0, far.shape[0], 512):
-            put_rows(table, near_rows // parts + first, 0.5 * dot(far[first : first + 512, :], inner[...]))
+        slots = far.shape[1]
+        for first in range(0, far.shape[0], 64):
+            values = dot(far[first : first + 64].reshape(64 * slots, width), inner[width : 2 * width, :])
+            put_rows(table, near_rows // parts + first * slots, 0.5 * values)
         table_load.wait()
         for piece in range(0, unit, PIECE):
             gather(0, rows[0], piece)
-        outer_load.wait()
 
     for u in range(units + 2):
         for piece in range(0, unit, PIECE):
@@ -315,8 +316,6 @@
 
     @pl.when(step == steps - 1)
     def _():
-        for load in node_loads:
-            load.wait()
         post[:nodes, :] = 0.5 * dot(incoming[...].astype(BF16), node_inner[...]) + node_part[...]
         for at in range(0, nodes, PIECE):
             hidden[at : at + PIECE, :] = half_silu(post[at : at + PIECE, :]).astype(BF16)
@@ -338,7 +337,6 @@
     block = 1024
     steps = edges // block
     all_units = edges // unit
-    hbm = pl.BlockSpec(memory_space=pltpu.HBM)
     vmem = pl.BlockSpec(memory_space=pltpu.VMEM)
     vector = pl.BlockSpec((1, width), lambda i, ids: (0, 0), pipeline_mode=pl.Buffered(1))
     return pl.pallas_call(
@@ -347,10 +345,10 @@
             num_scalar_prefetch=1,
             grid=(steps,),
             in_specs=[pl.BlockSpec((all_units, 1, unit), lambda i, ids: (0, 0, 0), pipeline_mode=pl.Buffered(1))]
-            + [vector] * 6 + [vmem] * 5 + [hbm] * 5,
+            + [vector] * 6 + [vmem] * 10,
             out_specs=[pl.BlockSpec(memory_space=pl.ANY), pl.BlockSpec((nodes, width), lambda i, ids: (0, 0))],
             scratch_shapes=[
-                pltpu.VMEM((table.shape[0] + far.shape[0] * parts, LANES), F32),
+                pltpu.VMEM((table.shape[0] + far.shape[0] * far.shape[1] * parts, LANES), F32),
                 pltpu.VMEM((nodes, width), F32),
                 pltpu.VMEM((block, width), BF16),
                 pltpu.VMEM((block, width), F32),
@@ -358,12 +356,7 @@
                 pltpu.VMEM((unit * parts, LANES), F32),
                 pltpu.VMEM((unit * parts, LANES), F32),
                 pltpu.VMEM((edges, width), BF16),
-                pltpu.VMEM((width, width), BF16),
-                pltpu.VMEM((width, width), BF16),
-                pltpu.VMEM((nodes, width), BF16),
-                pltpu.VMEM((width, width), BF16),
-                pltpu.VMEM((width, width), BF16),
-                pltpu.SemaphoreType.DMA((8,)),
+                pltpu.SemaphoreType.DMA((1,)),
                 pltpu.SemaphoreType.DMA((all_units,)),
             ],
         ),
@@ -391,16 +384,16 @@
         vectors = [
             v.reshape(1, -1) for v in (edge_offset, edge_gain, edge_shift, node_offset, node_gain, node_shift)
         ]
-        pre, edge_copy, far, table, node_part, sender = exchange(
+        *kept, sender = exchange(
             n_row, n_col, far_send.swapaxes(1, 2), near_send, edge_receiver, edge_sender.reshape(-1, LANES),
             node_lat, edge_lat, edge_inner, edge_bias.reshape(1, -1), node_inner, node_bias.reshape(1, -1),
+            edge_outer, node_outer,
         )
-        pre, edge_copy, table, node_part = [
-            pltpu.with_memory_space_constraint(array, pltpu.VMEM) for array in (pre, edge_copy, table, node_part)
-        ]
+        pre, edge_copy, far, *rest = [pltpu.with_memory_space_constraint(array, pltpu.VMEM) for array in kept]
+        table, node_part, inner, outer, nodes, node_low, node_out = rest
         edge_new, node_new = update(
-            sender.reshape(-1), edge_receiver, pre, edge_copy, node_lat, far.reshape(-1, width), table, node_part,
-            edge_inner, edge_outer, node_inner, node_outer, vectors,
+            sender.reshape(-1), edge_receiver, pre, edge_copy, nodes, far, table, node_part,
+            inner, outer, node_low, node_out, vectors,
         )
         return edge_new, node_new
 

time: 44.8 us -> 43 us (0.960)
  Pallas kernels: 43.9 us -> 42.2 us
    pallas_call x1, Pallas kernels: 16.1 us -> 14.4 us  [update(): pl.pallas_call(update_kernel, grid_spec=pltpu.PrefetchScalarGridSpec(num_...]
where the time goes in v6:
time: 43 us; the launch traced here: 42.8 us
  Pallas kernels  42.2 us (98%)
  between operations  0.64 us (1%)
    pallas_call x1, Pallas kernels, exchange(): pl.pallas_call(functools.partial(exchange_kernel, n_row, n_col, block), o...  27.8 us
    pallas_call x1, Pallas kernels, update(): pl.pallas_call(update_kernel, grid_spec=pltpu.PrefetchScalarGridSpec(num_...  14.4 us

profile of v6, /device:TPU:1, one launch (start us, length us, event | category | flops | bytes accessed | tf_op | source)
XLA Modules:
  0.0 42.8 jit_solution(7755724068991260977)
XLA Ops:
  0.6 27.8 %exchange.1 = (f32[4096,512]{1,0:T(8,128)S(1)}, bf16[4096,512]{1,0:T(8,128)(2,1)S(1)}, bf16[128,8,512]{2,1,0:T(8,128)(2,1)S(1)}, f32[2560,128]{1,0:T(8,128)S(1)}...) custom-call(s32[1,8,128]{2,1,0:T(8,128)} %bitcast.15, ...), custom_call_target="tpu_custom_call" | custom-call | tf_op jit(solution)/shard_map/exchange/pallas_call | solution.py:194
  28.4 14.4 %update.1 = (bf16[4096,512]{1,0:T(8,128)(2,1)}, bf16[512,512]{1,0:T(8,128)(2,1)}) custom-call(s32[4096]{0:T(1024)} %bitcast.14, s32[8,1,512]{2,1,0:T(1,128)} %bitcast.12, f32[1,512]{1,0:T(1,128)} %bitcast.18, f32[1,512]{1,0:T(1,128)} %bitcast.19, f32[1,512]{1,0:T(1,128)} %bitcast.20, f32[1,512]{1,0:T(1,128)} %bitcast.21, f32[1,512]{1,0:T(1,128)} %bitcast.22, ...), custom_call_target="tpu_custom_call" | custom-call | tf_op jit(solution)/shard_map/update/pallas_call | solution.py:342

commit v7 on v6

--- a/solution.py
+++ b/solution.py
@@ -204,7 +204,7 @@
             pltpu.VMEM(node_lat.shape, BF16),
             pltpu.VMEM((width, width), BF16),
             pltpu.VMEM(node_outer.shape, BF16),
-            jax.ShapeDtypeStruct(sender.shape, jnp.int32),
+            pltpu.VMEM(sender.shape, jnp.int32),
         ),
         in_specs=[hbm] * 12,
         out_specs=(vmem,) * 11,
@@ -237,10 +237,11 @@
 
 
 def update_kernel(
-    sender, receiver, edge_offset, edge_gain, edge_shift, node_offset, node_gain, node_shift,
-    pre, edge, far, near_table, node_part, inner, edge_outer, node, node_inner, node_outer,
+    receiver_hbm, edge_offset_hbm, edge_gain_hbm, edge_shift_hbm, node_offset_hbm, node_gain_hbm, node_shift_hbm,
+    sender_rows, pre, edge, far, near_table, node_part, inner, edge_outer, node, node_inner, node_outer,
     edge_new, node_new,
-    table, incoming, hidden, post, message, rows_a, rows_b, edge_out, load_sem, out_sem,
+    table, incoming, hidden, post, message, rows_a, rows_b, edge_out,
+    sender, receiver, edge_offset, edge_gain, edge_shift, node_offset, node_gain, node_shift, load_sem, out_sem,
 ):
     step, steps = pl.program_id(0), pl.num_programs(0)
     edges, width = edge.shape
@@ -253,6 +254,12 @@
 
     copy = pltpu.make_async_copy
     table_load = copy(near_table, table.at[pl.ds(0, near_rows)], load_sem.at[0])
+    sender_load = copy(sender_rows, sender, load_sem.at[1])
+    sources = (
+        receiver_hbm, edge_offset_hbm, edge_gain_hbm, edge_shift_hbm, node_offset_hbm, node_gain_hbm, node_shift_hbm,
+    )
+    targets = (receiver, edge_offset, edge_gain, edge_shift, node_offset, node_gain, node_shift)
+    small_loads = [copy(a, b, load_sem.at[2 + i]) for i, (a, b) in enumerate(zip(sources, targets))]
 
     def part_of(ref, u):
         return ref.at[pl.ds(pl.multiple_of(u * unit, unit), unit)]
@@ -260,9 +267,9 @@
     def edge_store(u):
         return copy(part_of(edge_out, u), part_of(edge_new, u), out_sem.at[u])
 
-    def gather(first, buffer, piece):
+    def gather(u, buffer, piece):
         for j in range(piece, piece + PIECE):
-            start = pl.multiple_of(sender[first + j], parts)
+            start = pl.multiple_of(sender[u * (unit // LANES) + j // LANES, j % LANES], parts)
             buffer[pl.ds(j * parts, parts), :] = table[pl.ds(start, parts), :]
 
     base = pl.multiple_of(step * (units * unit), units * unit)
@@ -289,22 +296,26 @@
 
     @pl.when(step == 0)
     def _():
-        table_load.start()
+        for load in [sender_load, table_load] + small_loads:
+            load.start()
         incoming[...] = jnp.zeros_like(incoming)
         slots = far.shape[1]
         for first in range(0, far.shape[0], 64):
             values = dot(far[first : first + 64].reshape(64 * slots, width), inner[width : 2 * width, :])
             put_rows(table, near_rows // parts + first * slots, 0.5 * values)
         table_load.wait()
+        sender_load.wait()
         for piece in range(0, unit, PIECE):
             gather(0, rows[0], piece)
+        for load in small_loads:
+            load.wait()
 
     for u in range(units + 2):
         for piece in range(0, unit, PIECE):
             if u < units:
                 activate(u, piece)
                 following = jnp.minimum(step * units + u + 1, all_units - 1)
-                gather(following * unit, rows[(u + 1) % 2], piece)
+                gather(following, rows[(u + 1) % 2], piece)
             if 1 <= u <= units:
                 finish(u - 1, piece)
         if u < units:
@@ -338,15 +349,13 @@
     steps = edges // block
     all_units = edges // unit
     vmem = pl.BlockSpec(memory_space=pltpu.VMEM)
-    vector = pl.BlockSpec((1, width), lambda i, ids: (0, 0), pipeline_mode=pl.Buffered(1))
+    hbm = pl.BlockSpec(memory_space=pltpu.HBM)
     return pl.pallas_call(
         update_kernel,
-        grid_spec=pltpu.PrefetchScalarGridSpec(
-            num_scalar_prefetch=1,
+        grid_spec=pl.GridSpec(
             grid=(steps,),
-            in_specs=[pl.BlockSpec((all_units, 1, unit), lambda i, ids: (0, 0, 0), pipeline_mode=pl.Buffered(1))]
-            + [vector] * 6 + [vmem] * 10,
-            out_specs=[pl.BlockSpec(memory_space=pl.ANY), pl.BlockSpec((nodes, width), lambda i, ids: (0, 0))],
+            in_specs=[hbm] * 7 + [vmem] * 11,
+            out_specs=[pl.BlockSpec(memory_space=pl.ANY), pl.BlockSpec((nodes, width), lambda i: (0, 0))],
             scratch_shapes=[
                 pltpu.VMEM((table.shape[0] + far.shape[0] * far.shape[1] * parts, LANES), F32),
                 pltpu.VMEM((nodes, width), F32),
@@ -356,7 +365,12 @@
                 pltpu.VMEM((unit * parts, LANES), F32),
                 pltpu.VMEM((unit * parts, LANES), F32),
                 pltpu.VMEM((edges, width), BF16),
-                pltpu.SemaphoreType.DMA((1,)),
+                pltpu.SMEM(sender.shape, jnp.int32),
+                pltpu.VMEM((all_units, 1, unit), jnp.int32),
+            ]
+            + [pltpu.VMEM((1, width), F32)] * 6
+            + [
+                pltpu.SemaphoreType.DMA((9,)),
                 pltpu.SemaphoreType.DMA((all_units,)),
             ],
         ),
@@ -367,8 +381,8 @@
         compiler_params=pltpu.CompilerParams(vmem_limit_bytes=UPDATE_BYTES),
         name="update",
     )(
-        sender, receiver.reshape(all_units, 1, unit), *vectors,
-        pre, edge_lat, far, table, node_part, inner, edge_outer, node_lat, node_inner, node_outer,
+        receiver.reshape(all_units, 1, unit), *vectors,
+        sender, pre, edge_lat, far, table, node_part, inner, edge_outer, node_lat, node_inner, node_outer,
     )
 
 
@@ -384,15 +398,15 @@
         vectors = [
             v.reshape(1, -1) for v in (edge_offset, edge_gain, edge_shift, node_offset, node_gain, node_shift)
         ]
-        *kept, sender = exchange(
+        kept = exchange(
             n_row, n_col, far_send.swapaxes(1, 2), near_send, edge_receiver, edge_sender.reshape(-1, LANES),
             node_lat, edge_lat, edge_inner, edge_bias.reshape(1, -1), node_inner, node_bias.reshape(1, -1),
             edge_outer, node_outer,
         )
         pre, edge_copy, far, *rest = [pltpu.with_memory_space_constraint(array, pltpu.VMEM) for array in kept]
-        table, node_part, inner, outer, nodes, node_low, node_out = rest
+        table, node_part, inner, outer, nodes, node_low, node_out, sender = rest
         edge_new, node_new = update(
-            sender.reshape(-1), edge_receiver, pre, edge_copy, nodes, far, table, node_part,
+            sender, edge_receiver, pre, edge_copy, nodes, far, table, node_part,
             inner, outer, node_low, node_out, vectors,
         )
         return edge_new, node_new

time: 43 us -> 40.9 us (0.951)
  Pallas kernels: 42.2 us -> 40.2 us
    pallas_call x1, Pallas kernels: 14.4 us -> 13 us  [update(): pl.pallas_call(update_kernel, grid_spec=pl.GridSpec(grid=(steps,), in_spe...]
    pallas_call x1, Pallas kernels: 27.8 us -> 27.1 us  [exchange(): pl.pallas_call(functools.partial(exchange_kernel, n_row, n_col, block), o...]
where the time goes in v7:
time: 40.9 us; the launch traced here: 40.8 us
  Pallas kernels  40.2 us (98%)
  between operations  0.64 us (2%)
    pallas_call x1, Pallas kernels, exchange(): pl.pallas_call(functools.partial(exchange_kernel, n_row, n_col, block), o...  27.1 us
    pallas_call x1, Pallas kernels, update(): pl.pallas_call(update_kernel, grid_spec=pl.GridSpec(grid=(steps,), in_spe...  13 us

profile of v7, /device:TPU:1, one launch (start us, length us, event | category | flops | bytes accessed | tf_op | source)
XLA Modules:
  0.0 40.8 jit_solution(1955573081776707599)
XLA Ops:
  0.6 27.1 %exchange.1 = (f32[4096,512]{1,0:T(8,128)S(1)}, bf16[4096,512]{1,0:T(8,128)(2,1)S(1)}, bf16[128,8,512]{2,1,0:T(8,128)(2,1)S(1)}, f32[2560,128]{1,0:T(8,128)S(1)}...) custom-call(s32[1,8,128]{2,1,0:T(8,128)} %bitcast.13, ...), custom_call_target="tpu_custom_call" | custom-call | tf_op jit(solution)/shard_map/exchange/pallas_call | solution.py:194
  27.8 13.0 %update.1 = (bf16[4096,512]{1,0:T(8,128)(2,1)}, bf16[512,512]{1,0:T(8,128)(2,1)}) custom-call(s32[8,1,512]{2,1,0:T(1,128)} %bitcast.11, f32[1,512]{1,0:T(1,128)} %bitcast.16, f32[1,512]{1,0:T(1,128)} %bitcast.17, f32[1,512]{1,0:T(1,128)} %bitcast.18, f32[1,512]{1,0:T(1,128)} %bitcast.19, f32[1,512]{1,0:T(1,128)} %bitcast.20, f32[1,512]{1,0:T(1,128)} %bitcast.21, ...), custom_call_target="tpu_custom_call" | custom-call | tf_op jit(solution)/shard_map/update/pallas_call | solution.py:353

commit v8 on v7

--- a/solution.py
+++ b/solution.py
@@ -288,11 +288,13 @@
         message[at : at + PIECE, :] = values
         edge_out[pl.ds(base + at, PIECE), :] = edge[pl.ds(base + at, PIECE), :] + values
 
-    def scatter(u):
-        ids = receiver[step * units + u].astype(jnp.int16)
+    def scatter():
         node_ids = lax.broadcasted_iota(jnp.int16, (nodes, unit), 0)
-        hot = jnp.where(node_ids == ids, jnp.bfloat16(1), jnp.bfloat16(0))
-        incoming[...] += dot(hot, message[u * unit : (u + 1) * unit, :])
+        hot = [
+            jnp.where(node_ids == receiver[step * units + u].astype(jnp.int16), jnp.bfloat16(1), jnp.bfloat16(0))
+            for u in range(units)
+        ]
+        incoming[...] += dot(jnp.concatenate(hot, axis=1), message[...])
 
     @pl.when(step == 0)
     def _():
@@ -310,7 +312,7 @@
         for load in small_loads:
             load.wait()
 
-    for u in range(units + 2):
+    for u in range(units + 1):
         for piece in range(0, unit, PIECE):
             if u < units:
                 activate(u, piece)
@@ -320,8 +322,7 @@
                 finish(u - 1, piece)
         if u < units:
             post[u * unit : (u + 1) * unit, :] = dot(hidden[u * unit : (u + 1) * unit, :], edge_outer[...])
-        if u >= 2:
-            scatter(u - 2)
+    scatter()
     for u in range(units):
         edge_store(step * units + u).start()
 

time: 40.9 us -> 40.9 us (level)
  no operation moved by 1% of the time
where the time goes in v8:
time: 40.9 us; the launch traced here: 40.8 us
  Pallas kernels  40.2 us (98%)
  between operations  0.64 us (2%)
    pallas_call x1, Pallas kernels, exchange(): pl.pallas_call(functools.partial(exchange_kernel, n_row, n_col, block), o...  27.1 us
    pallas_call x1, Pallas kernels, update(): pl.pallas_call(update_kernel, grid_spec=pl.GridSpec(grid=(steps,), in_spe...  13 us

profile of v8, /device:TPU:1, one launch (start us, length us, event | category | flops | bytes accessed | tf_op | source)
XLA Modules:
  0.0 40.8 jit_solution(4316542787639143169)
XLA Ops:
  0.6 27.1 %exchange.1 = (f32[4096,512]{1,0:T(8,128)S(1)}, bf16[4096,512]{1,0:T(8,128)(2,1)S(1)}, bf16[128,8,512]{2,1,0:T(8,128)(2,1)S(1)}, f32[2560,128]{1,0:T(8,128)S(1)}...) custom-call(s32[1,8,128]{2,1,0:T(8,128)} %bitcast.13, ...), custom_call_target="tpu_custom_call" | custom-call | tf_op jit(solution)/shard_map/exchange/pallas_call | solution.py:194
  27.8 13.0 %update.1 = (bf16[4096,512]{1,0:T(8,128)(2,1)}, bf16[512,512]{1,0:T(8,128)(2,1)}) custom-call(s32[8,1,512]{2,1,0:T(1,128)} %bitcast.11, f32[1,512]{1,0:T(1,128)} %bitcast.16, f32[1,512]{1,0:T(1,128)} %bitcast.17, f32[1,512]{1,0:T(1,128)} %bitcast.18, f32[1,512]{1,0:T(1,128)} %bitcast.19, f32[1,512]{1,0:T(1,128)} %bitcast.20, f32[1,512]{1,0:T(1,128)} %bitcast.21, ...), custom_call_target="tpu_custom_call" | custom-call | tf_op jit(solution)/shard_map/update/pallas_call | solution.py:354
